TPU v7x, 256 devices: a whole 4x4x8 slice. The times are simulated.
256 devices in a mesh: sec: 4 (over y_lo, core), mom: 8 (over x, y_hi), en: 8 (over z).
Axes of the slice: x: 4, y: 4 (y_hi: 2, y_lo: 2; y = y_hi * 2 + y_lo), z: 8, core: 2. Of those that a mesh axis runs over, the one named last changes fastest.
Arguments:
- green_blocks: bfloat16 [8, 64, 2, 128, 128], P('mom', ('sec', 'en')), may hold values from -6 to 6
- derivative: bfloat16 [3, 128, 128], replicated, may hold values from -0.5 to 0.5
- bare_phonon: float32 [4, 8, 2, 3, 3, 128], P('sec', 'mom'), may hold values from -4 to 4
- prior_polar: float32 [4, 8, 2, 3, 3, 128], P('sec', 'mom'), may hold values from -4 to 4
- offsets: int32 [4], replicated, may hold values from 1 to 2, as said below
- momenta: int32 [8, 8], replicated, may hold values from 0 to 7, as said below
Outputs:
- sigma: float32 [8, 64, 2, 128, 128], P('mom', ('sec', 'en'))
- polarization: float32 [4, 8, 3, 128], P('sec', 'mom')
Inputs may be any that keep to these rules, and one draw needn't show every extreme that they name: `offsets`: every mode's offset lies in 1 to 2; some mode's offset equals 2 and another mode's equals 1. momenta[k, k'] = p((k - k') mod 8) for a permutation p of the 8 phonon momenta.
All inputs are finite; a program needn't handle non-finite values.
Results may differ from a plain program's by a relative error of at most 0.014.
Values may be sent and summed in bfloat16 or wider, within the bound.
No kernel may reach another device: no remote copies, remote signals or barrier semaphores. Data moves between devices by JAX's collectives and lax.ppermute only.
A program may use at most 64 MiB of HBM per device.

v0:
```python
import math

import jax
import jax.numpy as jnp
from jax import lax
from jax.sharding import PartitionSpec as P


def passed_along(x, axis, by):
    peers = lax.axis_size(axis)
    pairs = [(i, i + by) for i in range(peers) if 0 <= i + by < peers]
    return lax.ppermute(x, axis, pairs)


def contract(former, latter):
    return jnp.sum(former[..., :, :, None, :] * latter[..., None, :, :, :], axis=-3)


def complex_product(former, latter):
    real_part = contract(former[..., 0, :, :, :], latter[..., 0, :, :, :]) - contract(
        former[..., 1, :, :, :], latter[..., 1, :, :, :]
    )
    imag_part = contract(former[..., 0, :, :, :], latter[..., 1, :, :, :]) + contract(
        former[..., 1, :, :, :], latter[..., 0, :, :, :]
    )
    return jnp.stack([real_part, imag_part], axis=-4)


def dyson_update(bare_phonon, prior_polar):
    return bare_phonon + complex_product(complex_product(bare_phonon, prior_polar), bare_phonon)


def flipped_products(blocks, derivative):
    flipped = jnp.einsum(
        "ktcbx,ixa->kticab", blocks, derivative, preferred_element_type=jnp.float32
    )
    sign_flip = jnp.array([1.0, -1.0], jnp.float32).reshape(1, 1, 1, 2, 1, 1)
    return (flipped * sign_flip).astype(jnp.bfloat16)


def mode_weights(chosen):
    real_part = chosen[:, :, 0]
    imag_part = chosen[:, :, 1]
    upper_part = jnp.stack([real_part, -imag_part], axis=2)
    lower_part = jnp.stack([imag_part, real_part], axis=2)
    return jnp.stack([upper_part, lower_part], axis=2)


def weighted_rows(weights, selected):
    mode_count = weights.shape[1]
    total = None
    for mode_index in range(mode_count):
        for part_index in range(2):
            for direction in range(3):
                factor = jnp.transpose(
                    weights[:, mode_index, :, part_index, direction, :, :], (0, 2, 1, 3)
                )
                slab = selected[direction, :, mode_index, part_index].astype(jnp.float32)
                term = factor[:, None, :, :, :, None] * slab[None, :, None, None, :, :]
                total = term if total is None else total + term
    return total.astype(jnp.bfloat16)


def point_terms(source, chosen, derivative, offsets, targets, levels, flipped):
    blocks = jnp.einsum(
        "iab,scbd->iscad", derivative, source, preferred_element_type=jnp.float32
    ).astype(jnp.bfloat16)
    mode_count = chosen.shape[1]
    selected = jnp.stack(
        [
            lax.dynamic_slice_in_dim(blocks, levels - offsets[mode_index], targets, 1)
            for mode_index in range(mode_count)
        ],
        axis=2,
    )
    weights = mode_weights(chosen)
    combined = weighted_rows(weights, selected)
    sigma_part = jnp.einsum(
        "ktjxab,jbd->ktxad", combined, derivative, preferred_element_type=jnp.float32
    )
    polar_part = jnp.einsum(
        "itmcab,kticab->kmia", selected, flipped, preferred_element_type=jnp.float32
    )
    return (sigma_part, polar_part)


def per_device(green_blocks, derivative, bare_phonon, prior_polar, offsets, momenta):
    points = green_blocks.shape[0]
    levels = green_blocks.shape[1]
    block_order = green_blocks.shape[-1]
    all_points = points * lax.axis_size("mom")
    all_levels = levels * lax.axis_size("sec") * lax.axis_size("en")
    phonon = dyson_update(bare_phonon, prior_polar)
    local_modes = phonon.shape[0]
    stacked = phonon.reshape((local_modes * points,) + phonon.shape[2:])
    gathered = lax.all_gather(stacked, ("sec", "mom"), axis=0, tiled=True)
    mode_count = gathered.shape[0] // all_points
    phonon_table = jnp.transpose(
        gathered.reshape((mode_count, all_points) + phonon.shape[2:]), (1, 0, 2, 3, 4, 5)
    )
    own_rows = lax.dynamic_slice_in_dim(momenta, lax.axis_index("mom") * points, points, 0)
    momentum_ids = lax.broadcasted_iota(jnp.int32, (points, all_points), 1)
    lower_rim = passed_along(green_blocks, ("sec", "en"), 1)
    travelling = jnp.concatenate([lower_rim, green_blocks], axis=1)
    targets = green_blocks.shape[1]
    flipped = flipped_products(green_blocks, derivative)
    initial = (
        jnp.zeros((points, targets, 2, block_order, block_order), jnp.float32),
        jnp.zeros((all_points, mode_count, 3, block_order), jnp.float32),
    )
    pieces = lax.all_gather(travelling, "mom", axis=0, tiled=True)

    def one_point(position, running):
        sigma_sum, polar_sum = running
        source = lax.dynamic_index_in_dim(pieces, position, 0, keepdims=False)
        column = lax.dynamic_index_in_dim(own_rows, position, 1, keepdims=False)
        onehot = (column[:, None] == momentum_ids).astype(jnp.float32)
        chosen = jnp.einsum(
            "kq,qmxija->kmxija", onehot, phonon_table, precision=lax.Precision.HIGHEST
        )
        sigma_part, polar_part = point_terms(
            source, chosen, derivative, offsets, targets, levels, flipped
        )
        polar_sum = polar_sum + jnp.einsum(
            "kq,kmia->qmia", onehot, polar_part, precision=lax.Precision.HIGHEST
        )
        return (sigma_sum + sigma_part, polar_sum)

    sigma_sum, polar_sum = lax.fori_loop(0, pieces.shape[0], one_point, initial)
    sigma_scale = 1.0 / math.sqrt(9.0 * mode_count * all_points)
    polar_scale = 1.0 / math.sqrt(float(all_points * all_levels * block_order))
    ordered = jnp.transpose(polar_sum, (1, 0, 2, 3))
    summed = lax.psum(ordered, ("sec", "mom", "en"))
    own_share = lax.dynamic_slice(
        summed,
        (lax.axis_index("sec") * local_modes, lax.axis_index("mom") * points, 0, 0),
        (local_modes, points, 3, block_order),
    )
    return (sigma_sum * sigma_scale, own_share * polar_scale)


def solution(mesh):
    return jax.shard_map(
        per_device,
        mesh=mesh,
        in_specs=(
            P("mom", ("sec", "en"), None, None, None),
            P(),
            P("sec", "mom", None, None, None, None),
            P("sec", "mom", None, None, None, None),
            P(),
            P(),
        ),
        out_specs=(P("mom", ("sec", "en"), None, None, None), P("sec", "mom", None, None)),
        check_vma=False,
    )
```

profile of v0, /device:TPU:1, one launch (start us, length us, event | category | flops | bytes accessed | tf_op | source)
XLA Modules:
  0.0 422.1 jit_solution(5566107944990981499)
XLA Ops:
  7.3 4.5 %collective-permute-start = (bf16[1,2,2,128,128]{4,3,2,1,0:T(8,128)(2,1)}, bf16[1,2,2,128,128]{4,3,2,1,0:T(8,128)(2,1)S(1)}, u32[]{:S(2)}, u32[]{:S(2)}) collective-permute-start(bf16[1,2,2,128,128]{4,3,2,1,0:T(8,128)(2,1)} %param.9), channel_id=1, source_target_pairs={{0,1},{1,2},{2,3},{3,4},{4,5},{5,6},{6,7},{7,64},{64,65},{65,66},{... | collective-permute-start | bytes 393224 | tf_op jit(solution)/shard_map/ppermute | solution.py:12
  11.8 7.9 %collective-permute-done = bf16[1,2,2,128,128]{4,3,2,1,0:T(8,128)(2,1)S(1)} collective-permute-done((bf16[1,2,2,128,128]{4,3,2,1,0:T(8,128)(2,1)}, bf16[1,2,2,128,128]{4,3,2,1,0:T(8,128)(2,1)S(1)}, u32[]{:S(2)}, u32[]{:S(2)}) %collective-permute-start) | collective-permute-done | bytes 131104 | tf_op jit(solution)/shard_map/ppermute | solution.py:12
  19.7 1.6 pad_maximum_fusion.1
  21.3 1.5 fusion.141
  30.5 69.0 %all-gather = f32[32,1,2,3,3,128]{5,2,4,3,1,0:T(2,128)S(1)} all-gather(f32[1,1,2,3,3,128]{5,2,4,3,1,0:T(2,128)S(1)} %copy.131), channel_id=2, replica_groups=mesh['sec'=4,'mom'=8,'en'=8] {'sec','mom'}, dimensions={0}, use_global_device_ids=true | all-gather | bytes 304128 | tf_op jit(solution)/shard_map/all_gather | solution.py:96
  100.7 235.9 %while.19 = (s32[]{:T(128)}, f32[1,2,2,128,128]{4,3,2,1,0:T(8,128)}, f32[8,4,3,128]{3,2,1,0:T(4,128)}, s32[1,8]{1,0:T(1,128)}, f32[8,4,2,3,3,128]{5,4,3,2,1,0:T(...) while((s32[]{:T(128)}, ...), condition=%wide.region_9.10_spmd.clone, body=%wide.region_8.9_spmd.clone.sunk | while | flops 167619600 | bytes 31974176 | solution.py:129
  100.7 1.3 constant_dynamic-slice_fusion.3
  105.8 1.4 convolution_convert_fusion.2
  123.1 6.8 %fusion.167 = f32[1,2,2,128,128]{4,3,2,1,0:T(8,128)} fusion(f32[2,128,128]{2,1,0:T(8,128)S(1)} %copy-done.12, f32[3,2,128]{2,0,1:T(4,128)S(1)} %get-tuple-element.669, f32[2,128,128]{2,1,0:T(8,128)S(1)} %copy-done.13, f32[3,2,128]{2,0,1:T(4,128)S(1)} %get-tuple-element.671, f32[2,128,128]{2,1,0:T(8,128)} %copy.209, ...), kind=kOutput, calls=%fused_computation.5.clone.1 | convolution fusion | flops 59899904 | bytes 3842049 | tf_op jit(solution)/shard_map/while/body/eval_jaxpr/ktjxab,jbd->ktxad/dot_general | solution.py:78
  129.9 1.3 constant_dynamic-slice_fusion.3
  135.0 1.4 convolution_convert_fusion.2
  152.4 7.1 %fusion.167 = f32[1,2,2,128,128]{4,3,2,1,0:T(8,128)} fusion(f32[2,128,128]{2,1,0:T(8,128)S(1)} %copy-done.12, f32[3,2,128]{2,0,1:T(4,128)S(1)} %get-tuple-element.669, f32[2,128,128]{2,1,0:T(8,128)S(1)} %copy-done.13, f32[3,2,128]{2,0,1:T(4,128)S(1)} %get-tuple-element.671, f32[2,128,128]{2,1,0:T(8,128)} %copy.209, ...), kind=kOutput, calls=%fused_computation.5.clone.1 | convolution fusion | flops 59899904 | bytes 3842049 | tf_op jit(solution)/shard_map/while/body/eval_jaxpr/ktjxab,jbd->ktxad/dot_general | solution.py:78
  159.4 1.3 constant_dynamic-slice_fusion.3
  164.5 1.4 convolution_convert_fusion.2
  181.9 7.1 %fusion.167 = f32[1,2,2,128,128]{4,3,2,1,0:T(8,128)} fusion(f32[2,128,128]{2,1,0:T(8,128)S(1)} %copy-done.12, f32[3,2,128]{2,0,1:T(4,128)S(1)} %get-tuple-element.669, f32[2,128,128]{2,1,0:T(8,128)S(1)} %copy-done.13, f32[3,2,128]{2,0,1:T(4,128)S(1)} %get-tuple-element.671, f32[2,128,128]{2,1,0:T(8,128)} %copy.209, ...), kind=kOutput, calls=%fused_computation.5.clone.1 | convolution fusion | flops 59899904 | bytes 3842049 | tf_op jit(solution)/shard_map/while/body/eval_jaxpr/ktjxab,jbd->ktxad/dot_general | solution.py:78
  189.0 1.3 constant_dynamic-slice_fusion.3
  194.1 1.3 convolution_convert_fusion.2
  211.4 7.1 %fusion.167 = f32[1,2,2,128,128]{4,3,2,1,0:T(8,128)} fusion(f32[2,128,128]{2,1,0:T(8,128)S(1)} %copy-done.12, f32[3,2,128]{2,0,1:T(4,128)S(1)} %get-tuple-element.669, f32[2,128,128]{2,1,0:T(8,128)S(1)} %copy-done.13, f32[3,2,128]{2,0,1:T(4,128)S(1)} %get-tuple-element.671, f32[2,128,128]{2,1,0:T(8,128)} %copy.209, ...), kind=kOutput, calls=%fused_computation.5.clone.1 | convolution fusion | flops 59899904 | bytes 3842049 | tf_op jit(solution)/shard_map/while/body/eval_jaxpr/ktjxab,jbd->ktxad/dot_general | solution.py:78
  218.5 1.3 constant_dynamic-slice_fusion.3
  223.6 1.4 convolution_convert_fusion.2
  240.9 7.1 %fusion.167 = f32[1,2,2,128,128]{4,3,2,1,0:T(8,128)} fusion(f32[2,128,128]{2,1,0:T(8,128)S(1)} %copy-done.12, f32[3,2,128]{2,0,1:T(4,128)S(1)} %get-tuple-element.669, f32[2,128,128]{2,1,0:T(8,128)S(1)} %copy-done.13, f32[3,2,128]{2,0,1:T(4,128)S(1)} %get-tuple-element.671, f32[2,128,128]{2,1,0:T(8,128)} %copy.209, ...), kind=kOutput, calls=%fused_computation.5.clone.1 | convolution fusion | flops 59899904 | bytes 3842049 | tf_op jit(solution)/shard_map/while/body/eval_jaxpr/ktjxab,jbd->ktxad/dot_general | solution.py:78
  248.0 1.3 constant_dynamic-slice_fusion.3
  253.1 1.4 convolution_convert_fusion.2
  270.5 7.1 %fusion.167 = f32[1,2,2,128,128]{4,3,2,1,0:T(8,128)} fusion(f32[2,128,128]{2,1,0:T(8,128)S(1)} %copy-done.12, f32[3,2,128]{2,0,1:T(4,128)S(1)} %get-tuple-element.669, f32[2,128,128]{2,1,0:T(8,128)S(1)} %copy-done.13, f32[3,2,128]{2,0,1:T(4,128)S(1)} %get-tuple-element.671, f32[2,128,128]{2,1,0:T(8,128)} %copy.209, ...), kind=kOutput, calls=%fused_computation.5.clone.1 | convolution fusion | flops 59899904 | bytes 3842049 | tf_op jit(solution)/shard_map/while/body/eval_jaxpr/ktjxab,jbd->ktxad/dot_general | solution.py:78
  277.5 1.3 constant_dynamic-slice_fusion.3
  282.6 1.4 convolution_convert_fusion.2
  300.0 7.1 %fusion.167 = f32[1,2,2,128,128]{4,3,2,1,0:T(8,128)} fusion(f32[2,128,128]{2,1,0:T(8,128)S(1)} %copy-done.12, f32[3,2,128]{2,0,1:T(4,128)S(1)} %get-tuple-element.669, f32[2,128,128]{2,1,0:T(8,128)S(1)} %copy-done.13, f32[3,2,128]{2,0,1:T(4,128)S(1)} %get-tuple-element.671, f32[2,128,128]{2,1,0:T(8,128)} %copy.209, ...), kind=kOutput, calls=%fused_computation.5.clone.1 | convolution fusion | flops 59899904 | bytes 3842049 | tf_op jit(solution)/shard_map/while/body/eval_jaxpr/ktjxab,jbd->ktxad/dot_general | solution.py:78
  307.1 1.3 constant_dynamic-slice_fusion.3
  312.1 1.4 convolution_convert_fusion.2
  329.5 7.1 %fusion.167 = f32[1,2,2,128,128]{4,3,2,1,0:T(8,128)} fusion(f32[2,128,128]{2,1,0:T(8,128)S(1)} %copy-done.12, f32[3,2,128]{2,0,1:T(4,128)S(1)} %get-tuple-element.669, f32[2,128,128]{2,1,0:T(8,128)S(1)} %copy-done.13, f32[3,2,128]{2,0,1:T(4,128)S(1)} %get-tuple-element.671, f32[2,128,128]{2,1,0:T(8,128)} %copy.209, ...), kind=kOutput, calls=%fused_computation.5.clone.1 | convolution fusion | flops 59899904 | bytes 3842049 | tf_op jit(solution)/shard_map/while/body/eval_jaxpr/ktjxab,jbd->ktxad/dot_general | solution.py:78
  337.4 75.5 %psum.7 = f32[4,8,3,128]{3,1,2,0:T(8,128)S(1)} all-reduce(f32[4,8,3,128]{3,1,2,0:T(8,128)S(1)} %bitcast.412), channel_id=1, replica_groups=mesh['sec'=4,'mom'=8,'en'=8] {'sec','mom','en'}, use_global_device_ids=true, to_apply=%region_10.11 | all-reduce | flops 12288 | bytes 98304 | tf_op jit(solution)/shard_map/psum | solution.py:133
  413.0 1.7 broadcast_multiply_fusion
  (592 shorter events, 160.6 us)
Async XLA Ops:
  7.2 92.9 %copy-start = (s32[8,8]{1,0:T(8,128)S(1)}, s32[8,8]{1,0:T(8,128)}, u32[]{:S(2)}) copy-start(s32[8,8]{1,0:T(8,128)} %param.14) | copy-start | bytes 772
  7.2 92.5 %copy-start.18 = (f32[2]{0:T(128)S(1)}, f32[2]{0:T(128)}, u32[]{:S(2)}) copy-start(f32[2]{0:T(128)} %constant.97.clone) | copy-start | bytes 28
  7.2 92.5 %copy-start.16 = (bf16[1,2,2,128,128]{4,3,2,1,0:T(8,128)(2,1)S(1)}, bf16[1,2,2,128,128]{4,3,2,1,0:T(8,128)(2,1)}, u32[]{:S(2)}) copy-start(bf16[1,2,2,128,128]{4,3,2,1,0:T(8,128)(2,1)} %param.9) | copy-start | bytes 393220
  7.2 92.5 %copy-start.1 = (bf16[3,128,128]{2,1,0:T(8,128)(2,1)S(1)}, bf16[3,128,128]{2,1,0:T(8,128)(2,1)}, u32[]{:S(2)}) copy-start(bf16[3,128,128]{2,1,0:T(8,128)(2,1)} %param.10) | copy-start | bytes 294916
  7.2 93.5 %all-gather.3.cloned.1.call-start = ((), (), s32[]{:S(2)}) async-start(), calls=%async_computation | async-start | bytes 2359296 | tf_op jit(solution)/shard_map/all_gather | solution.py:111
  7.3 12.4 %collective-permute-start = (bf16[1,2,2,128,128]{4,3,2,1,0:T(8,128)(2,1)}, bf16[1,2,2,128,128]{4,3,2,1,0:T(8,128)(2,1)S(1)}, u32[]{:S(2)}, u32[]{:S(2)}) collective-permute-start(bf16[1,2,2,128,128]{4,3,2,1,0:T(8,128)(2,1)} %param.9), channel_id=1, source_target_pairs={{0,1},{1,2},{2,3},{3,4},{4,5},{5,6},{6,7},{7,64},{64,65},{65,66},{... | collective-permute-start | bytes 393224 | tf_op jit(solution)/shard_map/ppermute | solution.py:12
  117.1 5.9 %copy-start.2 = (f32[2,128,128]{2,1,0:T(8,128)S(1)}, f32[2,128,128]{2,1,0:T(8,128)}, u32[]{:S(2)}) copy-start(f32[2,128,128]{2,1,0:T(8,128)} %copy.221) | copy-start | bytes 393220 | tf_op jit(solution)/shard_map/while
  117.2 5.9 %copy-start.3 = (f32[2,128,128]{2,1,0:T(8,128)S(1)}, f32[2,128,128]{2,1,0:T(8,128)}, u32[]{:S(2)}) copy-start(f32[2,128,128]{2,1,0:T(8,128)} %copy.222) | copy-start | bytes 393220 | tf_op jit(solution)/shard_map/while
  117.2 5.9 %copy-start.4 = (f32[2,128,128]{2,1,0:T(8,128)S(1)}, f32[2,128,128]{2,1,0:T(8,128)}, u32[]{:S(2)}) copy-start(f32[2,128,128]{2,1,0:T(8,128)} %copy.223) | copy-start | bytes 393220 | tf_op jit(solution)/shard_map/while
  117.2 5.9 %copy-start.5 = (f32[2,128,128]{2,1,0:T(8,128)S(1)}, f32[2,128,128]{2,1,0:T(8,128)}, u32[]{:S(2)}) copy-start(f32[2,128,128]{2,1,0:T(8,128)} %copy.224) | copy-start | bytes 393220 | tf_op jit(solution)/shard_map/while
  117.2 5.9 %copy-start.6 = (f32[2,128,128]{2,1,0:T(8,128)S(1)}, f32[2,128,128]{2,1,0:T(8,128)}, u32[]{:S(2)}) copy-start(f32[2,128,128]{2,1,0:T(8,128)} %copy.225) | copy-start | bytes 393220 | tf_op jit(solution)/shard_map/while
  117.2 5.9 %copy-start.7 = (f32[2,128,128]{2,1,0:T(8,128)S(1)}, f32[2,128,128]{2,1,0:T(8,128)}, u32[]{:S(2)}) copy-start(f32[2,128,128]{2,1,0:T(8,128)} %copy.226) | copy-start | bytes 393220 | tf_op jit(solution)/shard_map/while
  146.4 5.9 %copy-start.2 = (f32[2,128,128]{2,1,0:T(8,128)S(1)}, f32[2,128,128]{2,1,0:T(8,128)}, u32[]{:S(2)}) copy-start(f32[2,128,128]{2,1,0:T(8,128)} %copy.221) | copy-start | bytes 393220 | tf_op jit(solution)/shard_map/while
  146.4 5.9 %copy-start.3 = (f32[2,128,128]{2,1,0:T(8,128)S(1)}, f32[2,128,128]{2,1,0:T(8,128)}, u32[]{:S(2)}) copy-start(f32[2,128,128]{2,1,0:T(8,128)} %copy.222) | copy-start | bytes 393220 | tf_op jit(solution)/shard_map/while
  146.4 5.9 %copy-start.4 = (f32[2,128,128]{2,1,0:T(8,128)S(1)}, f32[2,128,128]{2,1,0:T(8,128)}, u32[]{:S(2)}) copy-start(f32[2,128,128]{2,1,0:T(8,128)} %copy.223) | copy-start | bytes 393220 | tf_op jit(solution)/shard_map/while
  146.4 5.9 %copy-start.5 = (f32[2,128,128]{2,1,0:T(8,128)S(1)}, f32[2,128,128]{2,1,0:T(8,128)}, u32[]{:S(2)}) copy-start(f32[2,128,128]{2,1,0:T(8,128)} %copy.224) | copy-start | bytes 393220 | tf_op jit(solution)/shard_map/while
  146.4 5.9 %copy-start.6 = (f32[2,128,128]{2,1,0:T(8,128)S(1)}, f32[2,128,128]{2,1,0:T(8,128)}, u32[]{:S(2)}) copy-start(f32[2,128,128]{2,1,0:T(8,128)} %copy.225) | copy-start | bytes 393220 | tf_op jit(solution)/shard_map/while
  146.4 5.9 %copy-start.7 = (f32[2,128,128]{2,1,0:T(8,128)S(1)}, f32[2,128,128]{2,1,0:T(8,128)}, u32[]{:S(2)}) copy-start(f32[2,128,128]{2,1,0:T(8,128)} %copy.226) | copy-start | bytes 393220 | tf_op jit(solution)/shard_map/while
  175.9 5.9 %copy-start.2 = (f32[2,128,128]{2,1,0:T(8,128)S(1)}, f32[2,128,128]{2,1,0:T(8,128)}, u32[]{:S(2)}) copy-start(f32[2,128,128]{2,1,0:T(8,128)} %copy.221) | copy-start | bytes 393220 | tf_op jit(solution)/shard_map/while
  175.9 5.9 %copy-start.3 = (f32[2,128,128]{2,1,0:T(8,128)S(1)}, f32[2,128,128]{2,1,0:T(8,128)}, u32[]{:S(2)}) copy-start(f32[2,128,128]{2,1,0:T(8,128)} %copy.222) | copy-start | bytes 393220 | tf_op jit(solution)/shard_map/while
  175.9 5.9 %copy-start.4 = (f32[2,128,128]{2,1,0:T(8,128)S(1)}, f32[2,128,128]{2,1,0:T(8,128)}, u32[]{:S(2)}) copy-start(f32[2,128,128]{2,1,0:T(8,128)} %copy.223) | copy-start | bytes 393220 | tf_op jit(solution)/shard_map/while
  175.9 5.9 %copy-start.5 = (f32[2,128,128]{2,1,0:T(8,128)S(1)}, f32[2,128,128]{2,1,0:T(8,128)}, u32[]{:S(2)}) copy-start(f32[2,128,128]{2,1,0:T(8,128)} %copy.224) | copy-start | bytes 393220 | tf_op jit(solution)/shard_map/while
  175.9 5.9 %copy-start.6 = (f32[2,128,128]{2,1,0:T(8,128)S(1)}, f32[2,128,128]{2,1,0:T(8,128)}, u32[]{:S(2)}) copy-start(f32[2,128,128]{2,1,0:T(8,128)} %copy.225) | copy-start | bytes 393220 | tf_op jit(solution)/shard_map/while
  176.0 5.9 %copy-start.7 = (f32[2,128,128]{2,1,0:T(8,128)S(1)}, f32[2,128,128]{2,1,0:T(8,128)}, u32[]{:S(2)}) copy-start(f32[2,128,128]{2,1,0:T(8,128)} %copy.226) | copy-start | bytes 393220 | tf_op jit(solution)/shard_map/while
  205.4 5.9 %copy-start.2 = (f32[2,128,128]{2,1,0:T(8,128)S(1)}, f32[2,128,128]{2,1,0:T(8,128)}, u32[]{:S(2)}) copy-start(f32[2,128,128]{2,1,0:T(8,128)} %copy.221) | copy-start | bytes 393220 | tf_op jit(solution)/shard_map/while
  205.4 5.9 %copy-start.3 = (f32[2,128,128]{2,1,0:T(8,128)S(1)}, f32[2,128,128]{2,1,0:T(8,128)}, u32[]{:S(2)}) copy-start(f32[2,128,128]{2,1,0:T(8,128)} %copy.222) | copy-start | bytes 393220 | tf_op jit(solution)/shard_map/while
  205.4 5.9 %copy-start.4 = (f32[2,128,128]{2,1,0:T(8,128)S(1)}, f32[2,128,128]{2,1,0:T(8,128)}, u32[]{:S(2)}) copy-start(f32[2,128,128]{2,1,0:T(8,128)} %copy.223) | copy-start | bytes 393220 | tf_op jit(solution)/shard_map/while
  205.5 5.9 %copy-start.5 = (f32[2,128,128]{2,1,0:T(8,128)S(1)}, f32[2,128,128]{2,1,0:T(8,128)}, u32[]{:S(2)}) copy-start(f32[2,128,128]{2,1,0:T(8,128)} %copy.224) | copy-start | bytes 393220 | tf_op jit(solution)/shard_map/while
  205.5 5.9 %copy-start.6 = (f32[2,128,128]{2,1,0:T(8,128)S(1)}, f32[2,128,128]{2,1,0:T(8,128)}, u32[]{:S(2)}) copy-start(f32[2,128,128]{2,1,0:T(8,128)} %copy.225) | copy-start | bytes 393220 | tf_op jit(solution)/shard_map/while
  205.5 5.9 %copy-start.7 = (f32[2,128,128]{2,1,0:T(8,128)S(1)}, f32[2,128,128]{2,1,0:T(8,128)}, u32[]{:S(2)}) copy-start(f32[2,128,128]{2,1,0:T(8,128)} %copy.226) | copy-start | bytes 393220 | tf_op jit(solution)/shard_map/while
  234.9 5.9 %copy-start.2 = (f32[2,128,128]{2,1,0:T(8,128)S(1)}, f32[2,128,128]{2,1,0:T(8,128)}, u32[]{:S(2)}) copy-start(f32[2,128,128]{2,1,0:T(8,128)} %copy.221) | copy-start | bytes 393220 | tf_op jit(solution)/shard_map/while
  235.0 5.9 %copy-start.3 = (f32[2,128,128]{2,1,0:T(8,128)S(1)}, f32[2,128,128]{2,1,0:T(8,128)}, u32[]{:S(2)}) copy-start(f32[2,128,128]{2,1,0:T(8,128)} %copy.222) | copy-start | bytes 393220 | tf_op jit(solution)/shard_map/while
  (94 other events, 303.5 us)
Sparse Core Ops, SparseCore 0:
  21.4 60.3 all-gather.2
where the time goes:
time: 428 us; the launch traced here: 422 us
  blocking collectives  145 us (34%)
  local copies, waits for them, and re-layouts  135 us (32%)
  matrix products  76.3 us (18%)
  other arithmetic  31.9 us (7%)
  between operations  19.4 us (5%)
  waiting for transfers between devices  7.91 us (2%)
  starting transfers between devices  4.53 us (1%)
    mul x192, local copies, waits for them, and re-layouts, weighted_rows(): term = factor[:, None, :, :, :, None] * slab[None, :, None, None, :, :]  108 us
    psum x1, blocking collectives, per_device(): summed = lax.psum(ordered, ('sec', 'mom', 'en'))  75.5 us
    all_gather x1, blocking collectives, per_device(): gathered = lax.all_gather(stacked, ('sec', 'mom'), axis=0, tiled=True)  69 us
    dot_general x8, matrix products, point_terms(): jnp.einsum('ktjxab,jbd->ktxad', combined, derivative, preferred_element_t...  56.2 us
    mul x40, other arithmetic, weighted_rows(): term = factor[:, None, :, :, :, None] * slab[None, :, None, None, :, :]  12.7 us
    dot_general x8, matrix products, point_terms(): jnp.einsum('iab,scbd->iscad', derivative, source, preferred_element_type=...  10.8 us
    dynamic_slice x8, local copies, waits for them, and re-layouts, one_point(): column = lax.dynamic_index_in_dim(own_rows, position, 1, keepdims=False)  10.7 us
    another operation x8, other arithmetic  10.2 us
  transfers between devices with their start and end apart: 2, of which 1 were waited for; matrix products, arithmetic and copies ran while one was open for 1% of the time, Pallas kernels for 0%

commit v1 on v0

v1 whole, which is shorter than its diff:
```python
import math

import jax
import jax.numpy as jnp
from jax import lax
from jax.experimental import pallas as pl
from jax.experimental.pallas import tpu as pltpu
from jax.sharding import PartitionSpec as P


NB = 128
BLK = 4 * NB
PH = 32
SHIFTS = [(dx, dy) for dx in range(4) for dy in range(2)]
OFFS = 2

VMEM = pl.BlockSpec(memory_space=pltpu.VMEM)
SMEM = pl.BlockSpec(memory_space=pltpu.SMEM)


def mom_pairs(dx, dy):
    return [(2 * x + y, 2 * ((x + dx) % 4) + (y ^ dy)) for x in range(4) for y in range(2)]


def cmul(former, latter):
    out = []
    for i in range(3):
        row = []
        for j in range(3):
            real = imag = None
            for m in range(3):
                fr, fi = former[i][m]
                lr, li = latter[m][j]
                rr = fr * lr - fi * li
                ii = fr * li + fi * lr
                real = rr if real is None else real + rr
                imag = ii if imag is None else imag + ii
            row.append((real, imag))
        out.append(row)
    return out


def prep_kernel(green_ref, bare_ref, prior_ref, payload_ref, rows_ref):
    for t in range(4):
        payload_ref[t * NB : (t + 1) * NB, :] = green_ref[t].T

    def entries(ref):
        return [[(ref[i, j, 0:1, :], ref[i, j, 1:2, :]) for j in range(3)] for i in range(3)]

    bare = entries(bare_ref)
    change = cmul(cmul(bare, entries(prior_ref)), bare)
    rows_ref[...] = jnp.zeros((PH, NB), jnp.float32)
    for x in range(2):
        for i in range(3):
            for j in range(3):
                at = x * 9 + i * 3 + j
                rows_ref[at : at + 1, :] = bare[i][j][x] + change[i][j][x]
    payload_ref[BLK : BLK + PH, :] = rows_ref[...].astype(jnp.bfloat16)


def side_by_side(deriv_ref):
    plain = jnp.concatenate([deriv_ref[i] for i in range(3)], axis=1)
    turned = jnp.concatenate([deriv_ref[i].T for i in range(3)], axis=1)
    return plain, turned


def place():
    me = lax.axis_index("mom")
    return me, me // 2, me % 2


def polar_rows(scale, which, mom_ref, deriv_ref, along_ref, across_ref, own, slots, out_ref, x_ref):
    plain, turned = side_by_side(deriv_ref)
    me, mx, my = place()
    last = lax.axis_index("en") == 7

    def target(e, x):
        rows = slice((e % 2 * 2 + x) * NB, (e % 2 * 2 + x + 1) * NB)
        block = own[rows, :] if e < 2 else jnp.where(last, across_ref[rows, :], along_ref[rows, :])
        return -block if x else block

    left = jnp.concatenate(
        [
            jnp.concatenate([target(e + off, x) for e in range(2) for x in range(2)], axis=1)
            for off in (1, 2)
        ],
        axis=0,
    )
    for n in range(len(which)):
        x_ref[n * 2 * NB : (n + 1) * 2 * NB, :] = jnp.dot(
            left, slots[n][:BLK, :], preferred_element_type=jnp.float32
        ).astype(jnp.bfloat16)
    plain32 = plain.astype(jnp.float32) * scale
    for n, s in enumerate(which):
        dx, dy = SHIFTS[s]
        z = jnp.dot(
            x_ref[n * 2 * NB : (n + 1) * 2 * NB, :], turned, preferred_element_type=jnp.float32
        )
        source = 2 * ((mx + 4 - dx) % 4) + (my + dy) % 2
        q = mom_ref[me, source]
        for off in range(OFFS):
            row = jnp.sum(z[off * NB : (off + 1) * NB, :] * plain32, axis=0, keepdims=True)
            for i in range(3):
                at = off * 3 + i
                out_ref[q, at : at + 1, :] = row[:, i * NB : (i + 1) * NB]


def early_kernel(scale, which, mom_ref, deriv_ref, along_ref, across_ref, *refs):
    slots, (out_ref, x_ref) = refs[: len(which)], refs[len(which) :]
    out_ref[...] = jnp.zeros(out_ref.shape, jnp.float32)
    polar_rows(scale, which, mom_ref, deriv_ref, along_ref, across_ref, slots[0], slots, out_ref, x_ref)


def late_kernel(scale, which, mom_ref, deriv_ref, along_ref, across_ref, sofar_ref, *refs):
    slots, (out_ref, phonon_ref, x_ref) = refs[:8], refs[8:]
    out_ref[...] = sofar_ref[...]
    for s in range(8):
        phonon_ref[s] = slots[s][BLK:, :]
    late = [slots[s] for s in which]
    polar_rows(scale, which, mom_ref, deriv_ref, along_ref, across_ref, slots[0], late, out_ref, x_ref)


def sigma_kernel(scale, mom_ref, off_ref, deriv_ref, *refs):
    slots = refs[:8]
    modes = refs[8:12]
    own_ref, rim_ref, w_ref, m_ref, acc_ref = refs[12:]
    _, turned = side_by_side(deriv_ref)
    me, mx, my = place()
    sec = lax.axis_index("sec")
    for off in range(OFFS):
        total = None
        for d in range(4):
            on = (off_ref[sec ^ d] == off + 1).astype(jnp.float32)
            term = modes[d][...].astype(jnp.float32) * on
            total = term if total is None else total + term
        w_ref[:, off] = total
    turned32 = turned.astype(jnp.float32)
    for s, (dx, dy) in enumerate(SHIFTS):
        source = 2 * ((mx + 4 - dx) % 4) + (my + dy) % 2
        q = mom_ref[me, source]
        at_slot = 2 * ((mx + 4 - q // 2) % 4) + (my + q) % 2
        for off in range(OFFS):
            w = w_ref[at_slot, off]
            for j in range(3):
                for x in range(2):
                    total = None
                    for i in range(3):
                        r = x * 9 + i * 3 + j
                        term = w[r : r + 1, :] * turned32[:, i * NB : (i + 1) * NB]
                        total = term if total is None else total + term
                    col = ((off * 3 + j) * 2 + x) * NB
                    m_ref[s * NB : (s + 1) * NB, col : col + NB] = total.astype(jnp.bfloat16)
        if s % 2 == 1:
            left = jnp.concatenate([slots[s - 1][:BLK, :], slots[s][:BLK, :]], axis=1)
            part = jnp.dot(
                left, m_ref[(s - 1) * NB : (s + 1) * NB, :], preferred_element_type=jnp.float32
            )
            if s == 1:
                acc_ref[...] = part
            else:
                acc_ref[...] += part

    def piece(e, y, off, j, x):
        col = ((off * 3 + j) * 2 + x) * NB
        row = (e * 2 + y) * NB
        return acc_ref[row : row + NB, col : col + NB]

    def combined(e, off, j):
        real = piece(e, 0, off, j, 0) - piece(e, 1, off, j, 1)
        imag = piece(e, 0, off, j, 1) + piece(e, 1, off, j, 0)
        return real, imag

    rows = []
    for j in range(3):
        a, b, c, d = combined(0, 0, j), combined(0, 1, j), combined(1, 0, j), combined(1, 1, j)
        rows.append(
            jnp.concatenate([a[0], a[1], b[0] + c[0], b[1] + c[1], d[0], d[1]], axis=1).astype(
                jnp.bfloat16
            )
        )
    right = jnp.concatenate(rows, axis=0)
    result = jnp.dot(turned, right, preferred_element_type=jnp.float32) * scale
    for x in range(2):
        own_ref[0, x] = jnp.zeros((NB, NB), jnp.float32)
        own_ref[1, x] = result[:, x * NB : (x + 1) * NB].T
    for t in range(4):
        col = (2 + t) * NB
        rim_ref[t // 2, t % 2] = result[:, col : col + NB].T.astype(jnp.bfloat16)


def finish_kernel(off_ref, parts_ref, out_ref):
    total = jnp.sum(parts_ref[...], axis=0)
    first = (off_ref[lax.axis_index("sec")] == 1).astype(jnp.float32)
    for i in range(3):
        out_ref[i] = total[i : i + 1] * first + total[3 + i : 4 + i] * (1.0 - first)


EARLY = (0, 1, 2, 6, 4)
LATE = (3, 7, 5)


def per_device(green_blocks, derivative, bare_phonon, prior_polar, offsets, momenta):
    levels = 64
    polar_scale = 1.0 / math.sqrt(8.0 * levels * NB)
    sigma_scale = 1.0 / math.sqrt(9.0 * 4 * 8)
    payload = pl.pallas_call(
        prep_kernel,
        out_shape=jax.ShapeDtypeStruct((BLK + PH, NB), jnp.bfloat16),
        in_specs=[VMEM] * 3,
        out_specs=VMEM,
        scratch_shapes=[pltpu.VMEM((PH, NB), jnp.float32)],
        name="prep",
    )(
        green_blocks.reshape(4, NB, NB),
        jnp.transpose(bare_phonon, (0, 1, 3, 4, 2, 5)).reshape(3, 3, 2, NB),
        jnp.transpose(prior_polar, (0, 1, 3, 4, 2, 5)).reshape(3, 3, 2, NB),
    )
    slots = [payload] + [None] * 7

    for s in (1, 2, 6, 4):
        slots[s] = lax.ppermute(payload, "mom", mom_pairs(*SHIFTS[s]))
    along = lax.ppermute(payload, "en", [(i, (i - 1) % 8) for i in range(8)])
    for s in (5, 3, 7):
        slots[s] = lax.ppermute(slots[1], "mom", mom_pairs(SHIFTS[s][0], 0))
    across = lax.ppermute(along, ("sec", "en"), [(8 * i + 15, 8 * i + 7) for i in range(3)])
    sofar = pl.pallas_call(
        lambda *refs: early_kernel(polar_scale, EARLY, *refs),
        out_shape=jax.ShapeDtypeStruct((8, 8, NB), jnp.float32),
        in_specs=[SMEM] + [VMEM] * (3 + len(EARLY)),
        out_specs=VMEM,
        scratch_shapes=[pltpu.VMEM((len(EARLY) * 2 * NB, NB), jnp.bfloat16)],
        cost_estimate=pl.CostEstimate(
            flops=1000000000, bytes_accessed=1000000, transcendentals=0
        ),
        name="early",
        compiler_params=pltpu.CompilerParams(vmem_limit_bytes=6 * 2**20),
    )(momenta, derivative, along, across, *[slots[s] for s in EARLY])
    polar, phonon = pl.pallas_call(
        lambda *refs: late_kernel(polar_scale, LATE, *refs),
        out_shape=(
            jax.ShapeDtypeStruct((8, 8, NB), jnp.float32),
            jax.ShapeDtypeStruct((8, PH, NB), jnp.bfloat16),
        ),
        in_specs=[SMEM] + [VMEM] * 12,
        out_specs=(VMEM, VMEM),
        scratch_shapes=[pltpu.VMEM((len(LATE) * 2 * NB, NB), jnp.bfloat16)],
        name="late",
        compiler_params=pltpu.CompilerParams(vmem_limit_bytes=6 * 2**20),
    )(momenta, derivative, along, across, sofar, *slots)
    by_point = lax.all_to_all(polar, "mom", 0, 0, tiled=True)
    modes = [phonon] + [
        lax.ppermute(phonon, "sec", [(i, i ^ d) for i in range(4)]) for d in (1, 2, 3)
    ]
    own, rim = pl.pallas_call(
        lambda *refs: sigma_kernel(sigma_scale, *refs),
        out_shape=(
            jax.ShapeDtypeStruct((2, 2, NB, NB), jnp.float32),
            jax.ShapeDtypeStruct((2, 2, NB, NB), jnp.bfloat16),
        ),
        in_specs=[SMEM, SMEM] + [VMEM] * 13,
        out_specs=(VMEM, VMEM),
        scratch_shapes=[
            pltpu.VMEM((8, OFFS, PH, NB), jnp.float32),
            pltpu.VMEM((8 * NB, 12 * NB), jnp.bfloat16),
            pltpu.VMEM((BLK, 12 * NB), jnp.float32),
        ],
        cost_estimate=pl.CostEstimate(flops=2000000000, bytes_accessed=2000000, transcendentals=0),
        name="sigma",
        compiler_params=pltpu.CompilerParams(vmem_limit_bytes=16 * 2**20),
    )(momenta, offsets, derivative, *slots, *modes)
    up = lax.ppermute(rim, "en", [(i, (i + 1) % 8) for i in range(8)])
    over = lax.ppermute(up, ("sec", "en"), [(8 * i, 8 * i + 8) for i in range(3)])
    mine = jnp.sum(by_point, axis=0)
    copies = jnp.broadcast_to(mine[None], (32,) + mine.shape)
    spread = lax.all_to_all(copies, ("sec", "en"), 0, 0, tiled=True)
    below = jnp.where(lax.axis_index("en") == 0, over, up)
    sigma = own + below.astype(jnp.float32)
    spread, sigma = lax.optimization_barrier((spread, sigma))
    polarization = pl.pallas_call(
        finish_kernel,
        out_shape=jax.ShapeDtypeStruct((3, 1, NB), jnp.float32),
        in_specs=[SMEM, VMEM],
        out_specs=VMEM,
        name="finish",
        compiler_params=pltpu.CompilerParams(vmem_limit_bytes=2 * 2**20),
    )(offsets, spread)
    polarization = jnp.transpose(polarization.reshape(1, 3, 1, NB), (0, 2, 1, 3))
    return sigma[None], polarization


def solution(mesh):
    return jax.shard_map(
        per_device,
        mesh=mesh,
        in_specs=(
            P("mom", ("sec", "en"), None, None, None),
            P(),
            P("sec", "mom", None, None, None, None),
            P("sec", "mom", None, None, None, None),
            P(),
            P(),
        ),
        out_specs=(P("mom", ("sec", "en"), None, None, None), P("sec", "mom", None, None)),
        check_vma=False,
    )
```

time: 428 us -> 74.4 us (0.17); the launches traced: 422 us -> 74.1 us
  blocking collectives: 145 us -> 9.59 us
  local copies, waits for them, and re-layouts: 135 us -> 1.58 us
  matrix products: 76.3 us -> 0 us
  other arithmetic: 31.9 us -> 0.76 us
  starting transfers between devices: 4.53 us -> 31.1 us
  between operations: 19.4 us -> 0.77 us
  waiting for transfers between devices: 7.91 us -> 21.7 us
  Pallas kernels: 0 us -> 8.55 us
    mul x192 -> x0, local copies, waits for them, and re-layouts: 108 us -> none  [weighted_rows(): term = factor[:, None, :, :, :, None] * slab[None, :, None, None, :, :]]
    dot_general x25 -> x0, matrix products: 76.3 us -> none  [the longest x8 56.2 us: point_terms(): jnp.einsum('ktjxab,jbd->ktxad', combined, derivative, preferred_element_t...]
    psum x1 -> x0, blocking collectives: 75.5 us -> none  [per_device(): summed = lax.psum(ordered, ('sec', 'mom', 'en'))]
    all_gather x1 -> x0, blocking collectives: 69 us -> none  [per_device(): gathered = lax.all_gather(stacked, ('sec', 'mom'), axis=0, tiled=True)]
    ppermute x1 -> x14, starting transfers between devices: 4.49 us -> 27.5 us  [the longest x4 7.12 us: per_device(): slots[s] = lax.ppermute(payload, 'mom', mom_pairs(*SHIFTS[s]))]
    mul x42 -> x0, other arithmetic: 15 us -> none  [the longest x40 12.7 us: weighted_rows(): term = factor[:, None, :, :, :, None] * slab[None, :, None, None, :, :]]
    dynamic_slice x9 -> x0, local copies, waits for them, and re-layouts: 11.2 us -> none  [the longest x8 10.7 us: one_point(): column = lax.dynamic_index_in_dim(own_rows, position, 1, keepdims=False)]
    while x257 -> x0, local copies, waits for them, and re-layouts: 10.9 us -> none
  transfers between devices with their start and end apart: 2 -> 15, of which waited for: 1 -> 6; matrix products, arithmetic and copies ran while one was open for 1% -> 2% of each run, Pallas kernels for 0% -> 2%
where the time goes in v1:
time: 74.4 us; the launch traced here: 74.1 us
  starting transfers between devices  31.1 us (42%)
  waiting for transfers between devices  21.7 us (29%)
  blocking collectives  9.59 us (13%)
  Pallas kernels  8.55 us (11%)
  local copies, waits for them, and re-layouts  1.58 us (2%)
  between operations  0.77 us (1%)
  other arithmetic  0.76 us (1%)
    all_to_all x1, blocking collectives, per_device(): by_point = lax.all_to_all(polar, 'mom', 0, 0, tiled=True)  9.59 us
    all_to_all x1, waiting for transfers between devices, per_device(): spread = lax.all_to_all(copies, ('sec', 'en'), 0, 0, tiled=True)  8.6 us
    ppermute x4, starting transfers between devices, per_device(): slots[s] = lax.ppermute(payload, 'mom', mom_pairs(*SHIFTS[s]))  7.12 us
    ppermute x1, waiting for transfers between devices, per_device(): up = lax.ppermute(rim, 'en', [(i, (i + 1) % 8) for i in range(8)])  6.76 us
    ppermute x1, starting transfers between devices, per_device(): along = lax.ppermute(payload, 'en', [(i, (i - 1) % 8) for i in range(8)])  6.39 us
    ppermute x3, starting transfers between devices, per_device(): slots[s] = lax.ppermute(slots[1], 'mom', mom_pairs(SHIFTS[s][0], 0))  5.87 us
    ppermute x3, starting transfers between devices, per_device(): lax.ppermute(phonon, 'sec', [(i, i ^ d) for i in range(4)])  4.19 us
    all_to_all x1, starting transfers between devices, per_device(): spread = lax.all_to_all(copies, ('sec', 'en'), 0, 0, tiled=True)  3.63 us
  transfers between devices with their start and end apart: 15, of which 6 were waited for; matrix products, arithmetic and copies ran while one was open for 2% of the time, Pallas kernels for 2%

profile of v1, /device:TPU:1, one launch (start us, length us, event | category | flops | bytes accessed | tf_op | source)
XLA Modules:
  0.0 74.1 jit_solution(10964011584920455025)
XLA Ops:
  0.7 1.7 %prep.1.refs_4_.refs_5_.refs_3_ = bf16[544,128]{1,0:T(8,128)(2,1)} custom-call(bf16[4,128,128]{2,1,0:T(8,128)(2,1)} %bitcast.12, f32[3,3,2,128]{3,2,1,0:T(2,128)} %bitcast.13, f32[3,3,2,128]{3,2,1,0:T(2,128)} %bitcast.14), custom_call_target="tpu_custom_call" | custom-call | tf_op jit(solution)/shard_map/prep/pallas_call | solution.py:206
  2.4 6.4 %collective-permute-start = (bf16[544,128]{1,0:T(8,128)(2,1)}, bf16[544,128]{1,0:T(8,128)(2,1)S(1)}, u32[]{:S(2)}, u32[]{:S(2)}) collective-permute-start(bf16[544,128]{1,0:T(8,128)(2,1)} %prep.1.refs_4_.refs_5_.refs_3_), channel_id=1, source_target_pairs={{0,7},{1,0},{2,1},{3,2},{4,3},{5,4},{6,5},{7,6},{8,15},{9,8},{10,9... | collective-permute-start | bytes 417800 | tf_op jit(solution)/shard_map/ppermute | solution.py:222
  8.8 2.9 %collective-permute-start.2 = (bf16[544,128]{1,0:T(8,128)(2,1)}, bf16[544,128]{1,0:T(8,128)(2,1)S(1)}, u32[]{:S(2)}, u32[]{:S(2)}) collective-permute-start(bf16[544,128]{1,0:T(8,128)(2,1)} %prep.1.refs_4_.refs_5_.refs_3_), channel_id=1, source_target_pairs={{0,8},{8,0},{16,24},{24,16},{32,40},{40,32},{48,56},{56,48},{1,9},... | collective-permute-start | bytes 417800 | tf_op jit(solution)/shard_map/ppermute | solution.py:221
  11.7 2.7 %collective-permute-start.5 = (bf16[544,128]{1,0:T(8,128)(2,1)}, bf16[544,128]{1,0:T(8,128)(2,1)S(1)}, u32[]{:S(2)}, u32[]{:S(2)}) collective-permute-start(bf16[544,128]{1,0:T(8,128)(2,1)} %prep.1.refs_4_.refs_5_.refs_3_), channel_id=1, source_target_pairs={{0,32},{8,40},{16,48},{24,56},{32,0},{40,8},{48,16},{56,24},{1,33}... | collective-permute-start | bytes 417800 | tf_op jit(solution)/shard_map/ppermute | solution.py:221
  14.4 0.9 %collective-permute-start.4 = (bf16[544,128]{1,0:T(8,128)(2,1)}, bf16[544,128]{1,0:T(8,128)(2,1)S(1)}, u32[]{:S(2)}, u32[]{:S(2)}) collective-permute-start(bf16[544,128]{1,0:T(8,128)(2,1)} %prep.1.refs_4_.refs_5_.refs_3_), channel_id=1, source_target_pairs={{0,48},{8,56},{16,0},{24,8},{32,16},{40,24},{48,32},{56,40},{1,49}... | collective-permute-start | bytes 417800 | tf_op jit(solution)/shard_map/ppermute | solution.py:221
  15.3 0.6 collective-permute-start.3
  15.9 0.7 collective-permute-start.1
  16.6 0.0 collective-permute-done.2.refs_5_.refs_6_.refs_4_
  16.6 2.1 %collective-permute-start.8 = (bf16[544,128]{1,0:T(8,128)(2,1)S(1)}, bf16[544,128]{1,0:T(8,128)(2,1)S(1)}, u32[]{:S(2)}, u32[]{:S(2)}) collective-permute-start(bf16[544,128]{1,0:T(8,128)(2,1)S(1)} %collective-permute-done.2.refs_5_.refs_6_.refs_4_), channel_id=1, source_target_pairs={{0,48},{8,56},{16,0},{24,8},{32,16},{40,24},{48,32},{56,40},{1,49}... | collective-permute-start | bytes 417800 | tf_op jit(solution)/shard_map/ppermute | solution.py:224
  18.7 1.4 %collective-permute-start.7 = (bf16[544,128]{1,0:T(8,128)(2,1)S(1)}, bf16[544,128]{1,0:T(8,128)(2,1)S(1)}, u32[]{:S(2)}, u32[]{:S(2)}) collective-permute-start(bf16[544,128]{1,0:T(8,128)(2,1)S(1)} %collective-permute-done.2.refs_5_.refs_6_.refs_4_), channel_id=1, source_target_pairs={{0,32},{8,40},{16,48},{24,56},{32,0},{40,8},{48,16},{56,24},{1,33}... | collective-permute-start | bytes 417800 | tf_op jit(solution)/shard_map/ppermute | solution.py:224
  20.1 0.3 collective-permute-done.4.refs_7_.refs_11_.refs_9_
  20.5 2.3 %collective-permute-start.6 = (bf16[544,128]{1,0:T(8,128)(2,1)S(1)}, bf16[544,128]{1,0:T(8,128)(2,1)S(1)}, u32[]{:S(2)}, u32[]{:S(2)}) collective-permute-start(bf16[544,128]{1,0:T(8,128)(2,1)S(1)} %collective-permute-done.2.refs_5_.refs_6_.refs_4_), channel_id=1, source_target_pairs={{0,16},{8,24},{16,32},{24,40},{32,48},{40,56},{48,0},{56,8},{1,17}... | collective-permute-start | bytes 417800 | tf_op jit(solution)/shard_map/ppermute | solution.py:224
  22.8 0.0 copy-start
  22.8 0.9 %copy-done = bf16[544,128]{1,0:T(8,128)(2,1)S(1)} copy-done((bf16[544,128]{1,0:T(8,128)(2,1)S(1)}, bf16[544,128]{1,0:T(8,128)(2,1)}, u32[]{:S(2)}) %copy-start) | copy-done | bytes 139288
  23.7 1.4 %early.1.refs_4_ = f32[8,8,128]{2,1,0:T(8,128)S(1)} custom-call(s32[8,8]{1,0:T(8,128)S(1)} %copy-done.3, bf16[3,128,128]{2,1,0:T(8,128)(2,1)S(1)} %copy-done.2, bf16[544,128]{1,0:T(8,128)(2,1)S(1)} %collective-permute-done.refs_2_, bf16[544,128]{1,0:T(8,128)(2,1)S(1)} %collective-permute-done.1.refs_3_, bf16[544,128]{1,0:T(8,128)(2,1)S(1)} %copy-done, ...), custom_call_target="tpu_custom_call" | custom-call | flops 1000000000 | bytes 1000000 | tf_op jit(solution)/shard_map/early/pallas_call | solution.py:226
  25.1 2.7 %collective-permute-done.6.refs_8_.refs_6_ = bf16[544,128]{1,0:T(8,128)(2,1)S(1)} collective-permute-done((bf16[544,128]{1,0:T(8,128)(2,1)S(1)}, bf16[544,128]{1,0:T(8,128)(2,1)S(1)}, u32[]{:S(2)}, u32[]{:S(2)}) %collective-permute-start.6) | collective-permute-done | bytes 139296 | tf_op jit(solution)/shard_map/ppermute | solution.py:224
  27.8 1.1 %late.1 = (f32[8,8,128]{2,1,0:T(8,128)S(1)}, bf16[8,32,128]{2,1,0:T(8,128)(2,1)S(1)}) custom-call(s32[8,8]{1,0:T(8,128)S(1)} %copy-done.3, bf16[3,128,128]{2,1,0:T(8,128)(2,1)S(1)} %copy-done.2, bf16[544,128]{1,0:T(8,128)(2,1)S(1)} %collective-permute-done.refs_2_, bf16[544,128]{1,0:T(8,128)(2,1)S(1)} %collective-permute-done.1.refs_3_, ...), custom_call_target="tpu_custom_call" | custom-call | tf_op jit(solution)/shard_map/late/pallas_call | solution.py:238
  28.9 0.0 copy-start.4
  28.9 3.1 %collective-permute-start.11 = (bf16[8,32,128]{2,1,0:T(8,128)(2,1)S(1)}, bf16[8,32,128]{2,1,0:T(8,128)(2,1)S(1)}, u32[]{:S(2)}, u32[]{:S(2)}) collective-permute-start(bf16[8,32,128]{2,1,0:T(8,128)(2,1)S(1)} %get-tuple-element.9.refs_11_), channel_id=1, source_target_pairs={{0,192},{64,128},{128,64},{192,0},{1,193},{65,129},{129,65},{193,1... | collective-permute-start | bytes 196616 | tf_op jit(solution)/shard_map/ppermute | solution.py:252
  32.0 1.1 %collective-permute-start.10 = (bf16[8,32,128]{2,1,0:T(8,128)(2,1)S(1)}, bf16[8,32,128]{2,1,0:T(8,128)(2,1)S(1)}, u32[]{:S(2)}, u32[]{:S(2)}) collective-permute-start(bf16[8,32,128]{2,1,0:T(8,128)(2,1)S(1)} %get-tuple-element.9.refs_11_), channel_id=1, source_target_pairs={{0,128},{64,192},{128,0},{192,64},{1,129},{65,193},{129,1},{193,65... | collective-permute-start | bytes 196616 | tf_op jit(solution)/shard_map/ppermute | solution.py:252
  33.1 0.9 %collective-permute-done.11.refs_14_ = bf16[8,32,128]{2,1,0:T(8,128)(2,1)S(1)} collective-permute-done((bf16[8,32,128]{2,1,0:T(8,128)(2,1)S(1)}, bf16[8,32,128]{2,1,0:T(8,128)(2,1)S(1)}, u32[]{:S(2)}, u32[]{:S(2)}) %collective-permute-start.11) | collective-permute-done | bytes 65568 | tf_op jit(solution)/shard_map/ppermute | solution.py:252
  34.0 2.4 %collective-permute-done.10.refs_13_ = bf16[8,32,128]{2,1,0:T(8,128)(2,1)S(1)} collective-permute-done((bf16[8,32,128]{2,1,0:T(8,128)(2,1)S(1)}, bf16[8,32,128]{2,1,0:T(8,128)(2,1)S(1)}, u32[]{:S(2)}, u32[]{:S(2)}) %collective-permute-start.10) | collective-permute-done | bytes 65568 | tf_op jit(solution)/shard_map/ppermute | solution.py:252
  36.4 3.2 %sigma.1 = (f32[2,2,128,128]{3,2,1,0:T(8,128)S(1)}, bf16[2,2,128,128]{3,2,1,0:T(8,128)(2,1)S(1)}) custom-call(s32[8,8]{1,0:T(8,128)S(1)} %copy-done.3, s32[4]{0:T(128)S(1)} %copy-done.4, bf16[3,128,128]{2,1,0:T(8,128)(2,1)S(1)} %copy-done.2, bf16[544,128]{1,0:T(8,128)(2,1)S(1)} %copy-done.1, ...), custom_call_target="tpu_custom_call" | custom-call | flops 2000000000 | bytes 2000000 | tf_op jit(solution)/shard_map/sigma/pallas_call | solution.py:254
  39.6 0.1 collective-permute-start.12
  39.7 6.8 %collective-permute-done.12 = bf16[2,2,128,128]{3,2,1,0:T(8,128)(2,1)S(1)} collective-permute-done((bf16[2,2,128,128]{3,2,1,0:T(8,128)(2,1)S(1)}, bf16[2,2,128,128]{3,2,1,0:T(8,128)(2,1)S(1)}, u32[]{:S(2)}, u32[]{:S(2)}) %collective-permute-start.12) | collective-permute-done | bytes 131104 | tf_op jit(solution)/shard_map/ppermute | solution.py:271
  46.5 3.2 %collective-permute-start.13 = (bf16[2,2,128,128]{3,2,1,0:T(8,128)(2,1)S(1)}, bf16[2,2,128,128]{3,2,1,0:T(8,128)(2,1)S(1)}, u32[]{:S(2)}, u32[]{:S(2)}) collective-permute-start(bf16[2,2,128,128]{3,2,1,0:T(8,128)(2,1)S(1)} %collective-permute-done.12), channel_id=1, source_target_pairs={{0,64},{64,128},{128,192},{8,72},{72,136},{136,200},{16,80},{80,14... | collective-permute-start | bytes 393224 | tf_op jit(solution)/shard_map/ppermute | solution.py:272
  49.7 9.6 %all_to_all.10 = f32[8,8,128]{2,1,0:T(8,128)S(1)} all-to-all(f32[8,8,128]{2,1,0:T(8,128)S(1)} %get-tuple-element.8), channel_id=1, replica_groups=mesh['sec'=4,'mom'=8,'en'=8] {'mom'}, dimensions={0} | all-to-all | bytes 65536 | tf_op jit(solution)/shard_map/all_to_all | solution.py:250
  59.3 0.7 broadcast_in_dim.4
  60.0 3.6 %all-to-all-start.1 = ((f32[32,8,128]{2,1,0:T(8,128)}), f32[32,8,128]{2,1,0:T(8,128)S(1)}, u32[]{:S(2)}, u32[]{:S(2)}) async-start(f32[32,8,128]{2,1,0:T(8,128)} %broadcast_in_dim.4), calls=%async_computation.1 | async-start | bytes 262144 | tf_op jit(solution)/shard_map/all_to_all | solution.py:275
  63.6 0.8 %convert_add_fusion = f32[2,2,128,128]{3,2,1,0:T(8,128)} fusion(f32[2,2,128,128]{3,2,1,0:T(8,128)S(1)} %get-tuple-element.10, bf16[2,2,128,128]{3,2,1,0:T(8,128)(2,1)S(1)} %collective-permute-done.13, bf16[2,2,128,128]{3,2,1,0:T(8,128)(2,1)S(1)} %collective-permute-done.12, pred[]{:T(512)S(6)} %eq.3), kind=kLoop, calls=%fused_computation | loop fusion | flops 196608 | bytes 786433 | tf_op jit(solution)/shard_map/add | solution.py:277
  64.4 8.6 %all-to-all-done.1.parts_ref = f32[32,8,128]{2,1,0:T(8,128)S(1)} async-done(((f32[32,8,128]{2,1,0:T(8,128)}), f32[32,8,128]{2,1,0:T(8,128)S(1)}, u32[]{:S(2)}, u32[]{:S(2)}) %all-to-all-start.1) | async-done | bytes 131104 | tf_op jit(solution)/shard_map/all_to_all | solution.py:275
  73.0 1.1 %finish.1 = f32[3,1,128]{2,1,0:T(1,128)} custom-call(s32[4]{0:T(128)S(1)} %copy-done.4, f32[32,8,128]{2,1,0:T(8,128)S(1)} %all-to-all-done.1.parts_ref), custom_call_target="tpu_custom_call" | custom-call | tf_op jit(solution)/shard_map/finish/pallas_call | solution.py:279
  (17 shorter events, 0.0 us)
Async XLA Ops:
  0.6 22.1 %copy-start.2 = (bf16[3,128,128]{2,1,0:T(8,128)(2,1)S(1)}, bf16[3,128,128]{2,1,0:T(8,128)(2,1)}, u32[]{:S(2)}) copy-start(bf16[3,128,128]{2,1,0:T(8,128)(2,1)} %refs_2_.1) | copy-start | bytes 294916
  0.6 22.1 %copy-start.3 = (s32[8,8]{1,0:T(8,128)S(1)}, s32[8,8]{1,0:T(8,128)}, u32[]{:S(2)}) copy-start(s32[8,8]{1,0:T(8,128)} %refs_0_.5) | copy-start | bytes 772
  2.4 13.5 %collective-permute-start = (bf16[544,128]{1,0:T(8,128)(2,1)}, bf16[544,128]{1,0:T(8,128)(2,1)S(1)}, u32[]{:S(2)}, u32[]{:S(2)}) collective-permute-start(bf16[544,128]{1,0:T(8,128)(2,1)} %prep.1.refs_4_.refs_5_.refs_3_), channel_id=1, source_target_pairs={{0,7},{1,0},{2,1},{3,2},{4,3},{5,4},{6,5},{7,6},{8,15},{9,8},{10,9... | collective-permute-start | bytes 417800 | tf_op jit(solution)/shard_map/ppermute | solution.py:222
  8.8 7.8 %collective-permute-start.2 = (bf16[544,128]{1,0:T(8,128)(2,1)}, bf16[544,128]{1,0:T(8,128)(2,1)S(1)}, u32[]{:S(2)}, u32[]{:S(2)}) collective-permute-start(bf16[544,128]{1,0:T(8,128)(2,1)} %prep.1.refs_4_.refs_5_.refs_3_), channel_id=1, source_target_pairs={{0,8},{8,0},{16,24},{24,16},{32,40},{40,32},{48,56},{56,48},{1,9},... | collective-permute-start | bytes 417800 | tf_op jit(solution)/shard_map/ppermute | solution.py:221
  11.7 7.0 %collective-permute-start.5 = (bf16[544,128]{1,0:T(8,128)(2,1)}, bf16[544,128]{1,0:T(8,128)(2,1)S(1)}, u32[]{:S(2)}, u32[]{:S(2)}) collective-permute-start(bf16[544,128]{1,0:T(8,128)(2,1)} %prep.1.refs_4_.refs_5_.refs_3_), channel_id=1, source_target_pairs={{0,32},{8,40},{16,48},{24,56},{32,0},{40,8},{48,16},{56,24},{1,33}... | collective-permute-start | bytes 417800 | tf_op jit(solution)/shard_map/ppermute | solution.py:221
  14.4 6.0 %collective-permute-start.4 = (bf16[544,128]{1,0:T(8,128)(2,1)}, bf16[544,128]{1,0:T(8,128)(2,1)S(1)}, u32[]{:S(2)}, u32[]{:S(2)}) collective-permute-start(bf16[544,128]{1,0:T(8,128)(2,1)} %prep.1.refs_4_.refs_5_.refs_3_), channel_id=1, source_target_pairs={{0,48},{8,56},{16,0},{24,8},{32,16},{40,24},{48,32},{56,40},{1,49}... | collective-permute-start | bytes 417800 | tf_op jit(solution)/shard_map/ppermute | solution.py:221
  15.3 7.5 %collective-permute-start.3 = (bf16[544,128]{1,0:T(8,128)(2,1)}, bf16[544,128]{1,0:T(8,128)(2,1)S(1)}, u32[]{:S(2)}, u32[]{:S(2)}) collective-permute-start(bf16[544,128]{1,0:T(8,128)(2,1)} %prep.1.refs_4_.refs_5_.refs_3_), channel_id=1, source_target_pairs={{0,16},{8,24},{16,32},{24,40},{32,48},{40,56},{48,0},{56,8},{1,17}... | collective-permute-start | bytes 417800 | tf_op jit(solution)/shard_map/ppermute | solution.py:221
  15.9 6.9 %collective-permute-start.1 = (bf16[544,128]{1,0:T(8,128)(2,1)S(1)}, bf16[544,128]{1,0:T(8,128)(2,1)S(1)}, u32[]{:S(2)}, u32[]{:S(2)}) collective-permute-start(bf16[544,128]{1,0:T(8,128)(2,1)S(1)} %collective-permute-done.refs_2_), channel_id=1, source_target_pairs={{71,7},{135,71},{199,135},{79,15},{143,79},{207,143},{87,23},{151,... | collective-permute-start | bytes 417800 | tf_op jit(solution)/shard_map/ppermute | solution.py:225
  16.6 8.5 %collective-permute-start.8 = (bf16[544,128]{1,0:T(8,128)(2,1)S(1)}, bf16[544,128]{1,0:T(8,128)(2,1)S(1)}, u32[]{:S(2)}, u32[]{:S(2)}) collective-permute-start(bf16[544,128]{1,0:T(8,128)(2,1)S(1)} %collective-permute-done.2.refs_5_.refs_6_.refs_4_), channel_id=1, source_target_pairs={{0,48},{8,56},{16,0},{24,8},{32,16},{40,24},{48,32},{56,40},{1,49}... | collective-permute-start | bytes 417800 | tf_op jit(solution)/shard_map/ppermute | solution.py:224
  18.7 6.4 %collective-permute-start.7 = (bf16[544,128]{1,0:T(8,128)(2,1)S(1)}, bf16[544,128]{1,0:T(8,128)(2,1)S(1)}, u32[]{:S(2)}, u32[]{:S(2)}) collective-permute-start(bf16[544,128]{1,0:T(8,128)(2,1)S(1)} %collective-permute-done.2.refs_5_.refs_6_.refs_4_), channel_id=1, source_target_pairs={{0,32},{8,40},{16,48},{24,56},{32,0},{40,8},{48,16},{56,24},{1,33}... | collective-permute-start | bytes 417800 | tf_op jit(solution)/shard_map/ppermute | solution.py:224
  20.5 7.3 %collective-permute-start.6 = (bf16[544,128]{1,0:T(8,128)(2,1)S(1)}, bf16[544,128]{1,0:T(8,128)(2,1)S(1)}, u32[]{:S(2)}, u32[]{:S(2)}) collective-permute-start(bf16[544,128]{1,0:T(8,128)(2,1)S(1)} %collective-permute-done.2.refs_5_.refs_6_.refs_4_), channel_id=1, source_target_pairs={{0,16},{8,24},{16,32},{24,40},{32,48},{40,56},{48,0},{56,8},{1,17}... | collective-permute-start | bytes 417800 | tf_op jit(solution)/shard_map/ppermute | solution.py:224
  22.8 0.9 %copy-start = (bf16[544,128]{1,0:T(8,128)(2,1)S(1)}, bf16[544,128]{1,0:T(8,128)(2,1)}, u32[]{:S(2)}) copy-start(bf16[544,128]{1,0:T(8,128)(2,1)} %prep.1.refs_4_.refs_5_.refs_3_) | copy-start | bytes 417796
  23.7 4.1 %copy-start.1 = (bf16[544,128]{1,0:T(8,128)(2,1)S(1)}, bf16[544,128]{1,0:T(8,128)(2,1)}, u32[]{:S(2)}) copy-start(bf16[544,128]{1,0:T(8,128)(2,1)} %prep.1.refs_4_.refs_5_.refs_3_) | copy-start | bytes 417796
  28.9 7.5 %copy-start.4 = (s32[4]{0:T(128)S(1)}, s32[4]{0:T(128)}, u32[]{:S(2)}) copy-start(s32[4]{0:T(128)} %off_ref.1) | copy-start | bytes 52
  28.9 5.1 %collective-permute-start.11 = (bf16[8,32,128]{2,1,0:T(8,128)(2,1)S(1)}, bf16[8,32,128]{2,1,0:T(8,128)(2,1)S(1)}, u32[]{:S(2)}, u32[]{:S(2)}) collective-permute-start(bf16[8,32,128]{2,1,0:T(8,128)(2,1)S(1)} %get-tuple-element.9.refs_11_), channel_id=1, source_target_pairs={{0,192},{64,128},{128,64},{192,0},{1,193},{65,129},{129,65},{193,1... | collective-permute-start | bytes 196616 | tf_op jit(solution)/shard_map/ppermute | solution.py:252
  32.0 4.4 %collective-permute-start.10 = (bf16[8,32,128]{2,1,0:T(8,128)(2,1)S(1)}, bf16[8,32,128]{2,1,0:T(8,128)(2,1)S(1)}, u32[]{:S(2)}, u32[]{:S(2)}) collective-permute-start(bf16[8,32,128]{2,1,0:T(8,128)(2,1)S(1)} %get-tuple-element.9.refs_11_), channel_id=1, source_target_pairs={{0,128},{64,192},{128,0},{192,64},{1,129},{65,193},{129,1},{193,65... | collective-permute-start | bytes 196616 | tf_op jit(solution)/shard_map/ppermute | solution.py:252
  33.1 3.3 %collective-permute-start.9 = (bf16[8,32,128]{2,1,0:T(8,128)(2,1)S(1)}, bf16[8,32,128]{2,1,0:T(8,128)(2,1)S(1)}, u32[]{:S(2)}, u32[]{:S(2)}) collective-permute-start(bf16[8,32,128]{2,1,0:T(8,128)(2,1)S(1)} %get-tuple-element.9.refs_11_), channel_id=1, source_target_pairs={{0,64},{64,0},{128,192},{192,128},{1,65},{65,1},{129,193},{193,129... | collective-permute-start | bytes 196616 | tf_op jit(solution)/shard_map/ppermute | solution.py:252
  39.6 6.9 %collective-permute-start.12 = (bf16[2,2,128,128]{3,2,1,0:T(8,128)(2,1)S(1)}, bf16[2,2,128,128]{3,2,1,0:T(8,128)(2,1)S(1)}, u32[]{:S(2)}, u32[]{:S(2)}) collective-permute-start(bf16[2,2,128,128]{3,2,1,0:T(8,128)(2,1)S(1)} %get-tuple-element.11), channel_id=1, source_target_pairs={{0,1},{1,2},{2,3},{3,4},{4,5},{5,6},{6,7},{7,0},{8,9},{9,10},{10,1... | collective-permute-start | bytes 393224 | tf_op jit(solution)/shard_map/ppermute | solution.py:271
  46.5 17.1 %collective-permute-start.13 = (bf16[2,2,128,128]{3,2,1,0:T(8,128)(2,1)S(1)}, bf16[2,2,128,128]{3,2,1,0:T(8,128)(2,1)S(1)}, u32[]{:S(2)}, u32[]{:S(2)}) collective-permute-start(bf16[2,2,128,128]{3,2,1,0:T(8,128)(2,1)S(1)} %collective-permute-done.12), channel_id=1, source_target_pairs={{0,64},{64,128},{128,192},{8,72},{72,136},{136,200},{16,80},{80,14... | collective-permute-start | bytes 393224 | tf_op jit(solution)/shard_map/ppermute | solution.py:272
  60.0 13.0 %all-to-all-start.1 = ((f32[32,8,128]{2,1,0:T(8,128)}), f32[32,8,128]{2,1,0:T(8,128)S(1)}, u32[]{:S(2)}, u32[]{:S(2)}) async-start(f32[32,8,128]{2,1,0:T(8,128)} %broadcast_in_dim.4), calls=%async_computation.1 | async-start | bytes 262144 | tf_op jit(solution)/shard_map/all_to_all | solution.py:275

commit v2 on v1

--- a/solution.py
+++ b/solution.py
@@ -69,9 +69,7 @@
     return me, me // 2, me % 2
 
 
-def polar_rows(scale, which, mom_ref, deriv_ref, along_ref, across_ref, own, slots, out_ref, x_ref):
-    plain, turned = side_by_side(deriv_ref)
-    me, mx, my = place()
+def targets_side(own, along_ref, across_ref):
     last = lax.axis_index("en") == 7
 
     def target(e, x):
@@ -79,18 +77,21 @@
         block = own[rows, :] if e < 2 else jnp.where(last, across_ref[rows, :], along_ref[rows, :])
         return -block if x else block
 
-    left = jnp.concatenate(
+    return jnp.concatenate(
         [
             jnp.concatenate([target(e + off, x) for e in range(2) for x in range(2)], axis=1)
             for off in (1, 2)
         ],
         axis=0,
     )
+
+
+def polar_rows(which, mom_ref, left, plain32, turned, slots, out_ref, x_ref):
+    me, mx, my = place()
     for n in range(len(which)):
         x_ref[n * 2 * NB : (n + 1) * 2 * NB, :] = jnp.dot(
             left, slots[n][:BLK, :], preferred_element_type=jnp.float32
         ).astype(jnp.bfloat16)
-    plain32 = plain.astype(jnp.float32) * scale
     for n, s in enumerate(which):
         dx, dy = SHIFTS[s]
         z = jnp.dot(
@@ -106,25 +107,31 @@
 
 
 def early_kernel(scale, which, mom_ref, deriv_ref, along_ref, across_ref, *refs):
-    slots, (out_ref, x_ref) = refs[: len(which)], refs[len(which) :]
+    slots, (out_ref, left_ref, plain_ref, turned_ref, x_ref) = refs[: len(which)], refs[len(which) :]
+    plain, turned = side_by_side(deriv_ref)
+    left = targets_side(slots[0], along_ref, across_ref)
+    plain32 = plain.astype(jnp.float32) * scale
+    left_ref[...] = left
+    plain_ref[...] = plain32
+    turned_ref[...] = turned
     out_ref[...] = jnp.zeros(out_ref.shape, jnp.float32)
-    polar_rows(scale, which, mom_ref, deriv_ref, along_ref, across_ref, slots[0], slots, out_ref, x_ref)
-
-
-def late_kernel(scale, which, mom_ref, deriv_ref, along_ref, across_ref, sofar_ref, *refs):
+    polar_rows(which, mom_ref, left, plain32, turned, slots, out_ref, x_ref)
+
+
+def late_kernel(which, mom_ref, sofar_ref, left_ref, plain_ref, turned_ref, *refs):
     slots, (out_ref, phonon_ref, x_ref) = refs[:8], refs[8:]
     out_ref[...] = sofar_ref[...]
     for s in range(8):
         phonon_ref[s] = slots[s][BLK:, :]
     late = [slots[s] for s in which]
-    polar_rows(scale, which, mom_ref, deriv_ref, along_ref, across_ref, slots[0], late, out_ref, x_ref)
-
-
-def sigma_kernel(scale, mom_ref, off_ref, deriv_ref, *refs):
+    polar_rows(which, mom_ref, left_ref[...], plain_ref[...], turned_ref[...], late, out_ref, x_ref)
+
+
+def sigma_kernel(scale, mom_ref, off_ref, turned_ref, *refs):
     slots = refs[:8]
     modes = refs[8:12]
     own_ref, rim_ref, w_ref, m_ref, acc_ref = refs[12:]
-    _, turned = side_by_side(deriv_ref)
+    turned = turned_ref[...]
     me, mx, my = place()
     sec = lax.axis_index("sec")
     for off in range(OFFS):
@@ -188,13 +195,6 @@
         rim_ref[t // 2, t % 2] = result[:, col : col + NB].T.astype(jnp.bfloat16)
 
 
-def finish_kernel(off_ref, parts_ref, out_ref):
-    total = jnp.sum(parts_ref[...], axis=0)
-    first = (off_ref[lax.axis_index("sec")] == 1).astype(jnp.float32)
-    for i in range(3):
-        out_ref[i] = total[i : i + 1] * first + total[3 + i : 4 + i] * (1.0 - first)
-
-
 EARLY = (0, 1, 2, 6, 4)
 LATE = (3, 7, 5)
 
@@ -223,11 +223,16 @@
     for s in (5, 3, 7):
         slots[s] = lax.ppermute(slots[1], "mom", mom_pairs(SHIFTS[s][0], 0))
     across = lax.ppermute(along, ("sec", "en"), [(8 * i + 15, 8 * i + 7) for i in range(3)])
-    sofar = pl.pallas_call(
+    sofar, left, plain, turned = pl.pallas_call(
         lambda *refs: early_kernel(polar_scale, EARLY, *refs),
-        out_shape=jax.ShapeDtypeStruct((8, 8, NB), jnp.float32),
+        out_shape=(
+            jax.ShapeDtypeStruct((8, 8, NB), jnp.float32),
+            jax.ShapeDtypeStruct((2 * NB, BLK), jnp.bfloat16),
+            jax.ShapeDtypeStruct((NB, 3 * NB), jnp.float32),
+            jax.ShapeDtypeStruct((NB, 3 * NB), jnp.bfloat16),
+        ),
         in_specs=[SMEM] + [VMEM] * (3 + len(EARLY)),
-        out_specs=VMEM,
+        out_specs=(VMEM,) * 4,
         scratch_shapes=[pltpu.VMEM((len(EARLY) * 2 * NB, NB), jnp.bfloat16)],
         cost_estimate=pl.CostEstimate(
             flops=1000000000, bytes_accessed=1000000, transcendentals=0
@@ -236,7 +241,7 @@
         compiler_params=pltpu.CompilerParams(vmem_limit_bytes=6 * 2**20),
     )(momenta, derivative, along, across, *[slots[s] for s in EARLY])
     polar, phonon = pl.pallas_call(
-        lambda *refs: late_kernel(polar_scale, LATE, *refs),
+        lambda *refs: late_kernel(LATE, *refs),
         out_shape=(
             jax.ShapeDtypeStruct((8, 8, NB), jnp.float32),
             jax.ShapeDtypeStruct((8, PH, NB), jnp.bfloat16),
@@ -246,7 +251,7 @@
         scratch_shapes=[pltpu.VMEM((len(LATE) * 2 * NB, NB), jnp.bfloat16)],
         name="late",
         compiler_params=pltpu.CompilerParams(vmem_limit_bytes=6 * 2**20),
-    )(momenta, derivative, along, across, sofar, *slots)
+    )(momenta, sofar, left, plain, turned, *slots)
     by_point = lax.all_to_all(polar, "mom", 0, 0, tiled=True)
     modes = [phonon] + [
         lax.ppermute(phonon, "sec", [(i, i ^ d) for i in range(4)]) for d in (1, 2, 3)
@@ -267,7 +272,7 @@
         cost_estimate=pl.CostEstimate(flops=2000000000, bytes_accessed=2000000, transcendentals=0),
         name="sigma",
         compiler_params=pltpu.CompilerParams(vmem_limit_bytes=16 * 2**20),
-    )(momenta, offsets, derivative, *slots, *modes)
+    )(momenta, offsets, turned, *slots, *modes)
     up = lax.ppermute(rim, "en", [(i, (i + 1) % 8) for i in range(8)])
     over = lax.ppermute(up, ("sec", "en"), [(8 * i, 8 * i + 8) for i in range(3)])
     mine = jnp.sum(by_point, axis=0)
@@ -276,15 +281,9 @@
     below = jnp.where(lax.axis_index("en") == 0, over, up)
     sigma = own + below.astype(jnp.float32)
     spread, sigma = lax.optimization_barrier((spread, sigma))
-    polarization = pl.pallas_call(
-        finish_kernel,
-        out_shape=jax.ShapeDtypeStruct((3, 1, NB), jnp.float32),
-        in_specs=[SMEM, VMEM],
-        out_specs=VMEM,
-        name="finish",
-        compiler_params=pltpu.CompilerParams(vmem_limit_bytes=2 * 2**20),
-    )(offsets, spread)
-    polarization = jnp.transpose(polarization.reshape(1, 3, 1, NB), (0, 2, 1, 3))
+    total = jnp.sum(spread, axis=0)
+    first = lax.dynamic_index_in_dim(offsets, lax.axis_index("sec"), 0, keepdims=False) == 1
+    polarization = jnp.where(first, total[0:3], total[3:6])[None, None]
     return sigma[None], polarization
 
 

time: 74.4 us -> 75 us (level)
  starting transfers between devices: 31.1 us -> 28.3 us
  blocking collectives: 9.59 us -> 11.6 us
  local copies, waits for them, and re-layouts: 1.58 us -> 2.76 us
  Pallas kernels: 8.55 us -> 7.54 us
    ppermute x3, starting transfers between devices: 5.87 us -> 3.54 us  [per_device(): slots[s] = lax.ppermute(slots[1], 'mom', mom_pairs(SHIFTS[s][0], 0))]
    all_to_all x1, blocking collectives: 9.59 us -> 11.6 us  [per_device(): by_point = lax.all_to_all(polar, 'mom', 0, 0, tiled=True)]
    ppermute x4, waiting for transfers between devices: 0.33 us -> 1.65 us  [per_device(): slots[s] = lax.ppermute(payload, 'mom', mom_pairs(*SHIFTS[s]))]
    pallas_call x2 -> x1, Pallas kernels: 2.28 us -> 1.12 us  [per_device(): pl.pallas_call(lambda *refs: late_kernel(LATE, *refs), out_shape=(jax.Sha...]
    all_to_all x1, waiting for transfers between devices: 8.6 us -> 7.55 us  [per_device(): spread = lax.all_to_all(copies, ('sec', 'en'), 0, 0, tiled=True)]
    ppermute x3, waiting for transfers between devices: 2.68 us -> 3.68 us  [per_device(): slots[s] = lax.ppermute(slots[1], 'mom', mom_pairs(SHIFTS[s][0], 0))]
  transfers between devices with their start and end apart: 15 -> 15, of which waited for: 6 -> 6; matrix products, arithmetic and copies ran while one was open for 2% -> 3% of each run, Pallas kernels for 2% -> 2%
where the time goes in v2:
time: 75 us; the launch traced here: 74.8 us
  starting transfers between devices  28.3 us (38%)
  waiting for transfers between devices  22.4 us (30%)
  blocking collectives  11.6 us (15%)
  Pallas kernels  7.54 us (10%)
  local copies, waits for them, and re-layouts  2.76 us (4%)
  between operations  1.41 us (2%)
  other arithmetic  0.81 us (1%)
    all_to_all x1, blocking collectives, per_device(): by_point = lax.all_to_all(polar, 'mom', 0, 0, tiled=True)  11.6 us
    all_to_all x1, waiting for transfers between devices, per_device(): spread = lax.all_to_all(copies, ('sec', 'en'), 0, 0, tiled=True)  7.55 us
    ppermute x4, starting transfers between devices, per_device(): slots[s] = lax.ppermute(payload, 'mom', mom_pairs(*SHIFTS[s]))  7.12 us
    ppermute x1, starting transfers between devices, per_device(): along = lax.ppermute(payload, 'en', [(i, (i - 1) % 8) for i in range(8)])  6.39 us
    ppermute x1, waiting for transfers between devices, per_device(): up = lax.ppermute(rim, 'en', [(i, (i + 1) % 8) for i in range(8)])  6.16 us
    ppermute x3, waiting for transfers between devices, per_device(): slots[s] = lax.ppermute(slots[1], 'mom', mom_pairs(SHIFTS[s][0], 0))  3.68 us
    all_to_all x1, starting transfers between devices, per_device(): spread = lax.all_to_all(copies, ('sec', 'en'), 0, 0, tiled=True)  3.64 us
    ppermute x3, starting transfers between devices, per_device(): slots[s] = lax.ppermute(slots[1], 'mom', mom_pairs(SHIFTS[s][0], 0))  3.54 us
  transfers between devices with their start and end apart: 15, of which 6 were waited for; matrix products, arithmetic and copies ran while one was open for 3% of the time, Pallas kernels for 2%

profile of v2, /device:TPU:1, one launch (start us, length us, event | category | flops | bytes accessed | tf_op | source)
XLA Modules:
  0.0 74.8 jit_solution(3749496659321085733)
XLA Ops:
  0.7 1.7 %prep.1.refs_4_.refs_5_.refs_3_ = bf16[544,128]{1,0:T(8,128)(2,1)} custom-call(bf16[4,128,128]{2,1,0:T(8,128)(2,1)} %bitcast.10, f32[3,3,2,128]{3,2,1,0:T(2,128)} %bitcast.11, f32[3,3,2,128]{3,2,1,0:T(2,128)} %bitcast.12), custom_call_target="tpu_custom_call" | custom-call | tf_op jit(solution)/shard_map/prep/pallas_call | solution.py:206
  2.4 6.4 %collective-permute-start = (bf16[544,128]{1,0:T(8,128)(2,1)}, bf16[544,128]{1,0:T(8,128)(2,1)S(1)}, u32[]{:S(2)}, u32[]{:S(2)}) collective-permute-start(bf16[544,128]{1,0:T(8,128)(2,1)} %prep.1.refs_4_.refs_5_.refs_3_), channel_id=1, source_target_pairs={{0,7},{1,0},{2,1},{3,2},{4,3},{5,4},{6,5},{7,6},{8,15},{9,8},{10,9... | collective-permute-start | bytes 417800 | tf_op jit(solution)/shard_map/ppermute | solution.py:222
  8.8 2.9 %collective-permute-start.2 = (bf16[544,128]{1,0:T(8,128)(2,1)}, bf16[544,128]{1,0:T(8,128)(2,1)S(1)}, u32[]{:S(2)}, u32[]{:S(2)}) collective-permute-start(bf16[544,128]{1,0:T(8,128)(2,1)} %prep.1.refs_4_.refs_5_.refs_3_), channel_id=1, source_target_pairs={{0,8},{8,0},{16,24},{24,16},{32,40},{40,32},{48,56},{56,48},{1,9},... | collective-permute-start | bytes 417800 | tf_op jit(solution)/shard_map/ppermute | solution.py:221
  11.7 1.2 %collective-permute-start.3 = (bf16[544,128]{1,0:T(8,128)(2,1)}, bf16[544,128]{1,0:T(8,128)(2,1)S(1)}, u32[]{:S(2)}, u32[]{:S(2)}) collective-permute-start(bf16[544,128]{1,0:T(8,128)(2,1)} %prep.1.refs_4_.refs_5_.refs_3_), channel_id=1, source_target_pairs={{0,16},{8,24},{16,32},{24,40},{32,48},{40,56},{48,0},{56,8},{1,17}... | collective-permute-start | bytes 417800 | tf_op jit(solution)/shard_map/ppermute | solution.py:221
  12.9 1.5 %collective-permute-start.4 = (bf16[544,128]{1,0:T(8,128)(2,1)}, bf16[544,128]{1,0:T(8,128)(2,1)S(1)}, u32[]{:S(2)}, u32[]{:S(2)}) collective-permute-start(bf16[544,128]{1,0:T(8,128)(2,1)} %prep.1.refs_4_.refs_5_.refs_3_), channel_id=1, source_target_pairs={{0,48},{8,56},{16,0},{24,8},{32,16},{40,24},{48,32},{56,40},{1,49}... | collective-permute-start | bytes 417800 | tf_op jit(solution)/shard_map/ppermute | solution.py:221
  14.3 1.5 %collective-permute-start.5 = (bf16[544,128]{1,0:T(8,128)(2,1)}, bf16[544,128]{1,0:T(8,128)(2,1)S(1)}, u32[]{:S(2)}, u32[]{:S(2)}) collective-permute-start(bf16[544,128]{1,0:T(8,128)(2,1)} %prep.1.refs_4_.refs_5_.refs_3_), channel_id=1, source_target_pairs={{0,32},{8,40},{16,48},{24,56},{32,0},{40,8},{48,16},{56,24},{1,33}... | collective-permute-start | bytes 417800 | tf_op jit(solution)/shard_map/ppermute | solution.py:221
  15.9 0.7 collective-permute-start.1
  16.6 0.4 collective-permute-start.6
  17.0 0.0 collective-permute-done.3.refs_6_.refs_7_.refs_5_
  17.0 1.8 %collective-permute-start.7 = (bf16[544,128]{1,0:T(8,128)(2,1)S(1)}, bf16[544,128]{1,0:T(8,128)(2,1)S(1)}, u32[]{:S(2)}, u32[]{:S(2)}) collective-permute-start(bf16[544,128]{1,0:T(8,128)(2,1)S(1)} %collective-permute-done.2.refs_5_.refs_6_.refs_4_), channel_id=1, source_target_pairs={{0,32},{8,40},{16,48},{24,56},{32,0},{40,8},{48,16},{56,24},{1,33}... | collective-permute-start | bytes 417800 | tf_op jit(solution)/shard_map/ppermute | solution.py:224
  18.8 1.3 %collective-permute-start.8 = (bf16[544,128]{1,0:T(8,128)(2,1)S(1)}, bf16[544,128]{1,0:T(8,128)(2,1)S(1)}, u32[]{:S(2)}, u32[]{:S(2)}) collective-permute-start(bf16[544,128]{1,0:T(8,128)(2,1)S(1)} %collective-permute-done.2.refs_5_.refs_6_.refs_4_), channel_id=1, source_target_pairs={{0,48},{8,56},{16,0},{24,8},{32,16},{40,24},{48,32},{56,40},{1,49}... | collective-permute-start | bytes 417800 | tf_op jit(solution)/shard_map/ppermute | solution.py:224
  20.2 1.6 %collective-permute-done.5.refs_8_.refs_9_.refs_7_ = bf16[544,128]{1,0:T(8,128)(2,1)S(1)} collective-permute-done((bf16[544,128]{1,0:T(8,128)(2,1)}, bf16[544,128]{1,0:T(8,128)(2,1)S(1)}, u32[]{:S(2)}, u32[]{:S(2)}) %collective-permute-start.5) | collective-permute-done | bytes 139296 | tf_op jit(solution)/shard_map/ppermute | solution.py:221
  21.8 0.9 %copy-done = bf16[544,128]{1,0:T(8,128)(2,1)S(1)} copy-done((bf16[544,128]{1,0:T(8,128)(2,1)S(1)}, bf16[544,128]{1,0:T(8,128)(2,1)}, u32[]{:S(2)}) %copy-start) | copy-done | bytes 139288
  22.7 1.4 %early.1 = (f32[8,8,128]{2,1,0:T(8,128)S(1)}, bf16[256,512]{1,0:T(8,128)(2,1)S(1)}, f32[128,384]{1,0:T(8,128)S(1)}, bf16[128,384]{1,0:T(8,128)(2,1)S(1)}) custom-call(s32[8,8]{1,0:T(8,128)S(1)} %copy-done.2, bf16[3,128,128]{2,1,0:T(8,128)(2,1)S(1)} %copy-done.3, bf16[544,128]{1,0:T(8,128)(2,1)S(1)} %collective-permute-done.refs_2_, ...), custom_call_target="tpu_custom_call" | custom-call | flops 1000000000 | bytes 1000000 | tf_op jit(solution)/shard_map/early/pallas_call | solution.py:226
  24.1 0.6 collective-permute-done.6.refs_8_.refs_6_
  24.7 3.1 %collective-permute-done.7.refs_10_.refs_8_ = bf16[544,128]{1,0:T(8,128)(2,1)S(1)} collective-permute-done((bf16[544,128]{1,0:T(8,128)(2,1)S(1)}, bf16[544,128]{1,0:T(8,128)(2,1)S(1)}, u32[]{:S(2)}, u32[]{:S(2)}) %collective-permute-start.7) | collective-permute-done | bytes 139296 | tf_op jit(solution)/shard_map/ppermute | solution.py:224
  27.7 1.1 %late.1 = (f32[8,8,128]{2,1,0:T(8,128)S(1)}, bf16[8,32,128]{2,1,0:T(8,128)(2,1)S(1)}) custom-call(s32[8,8]{1,0:T(8,128)S(1)} %copy-done.2, f32[8,8,128]{2,1,0:T(8,128)S(1)} %get-tuple-element.12.refs_1_, bf16[256,512]{1,0:T(8,128)(2,1)S(1)} %get-tuple-element.13.refs_2_, f32[128,384]{1,0:T(8,128)S(1)} %get-tuple-element.14.refs_3_, ...), custom_call_target="tpu_custom_call" | custom-call | tf_op jit(solution)/shard_map/late/pallas_call | solution.py:243
  28.9 0.0 copy-start.4
  28.9 0.5 collective-permute-start.10
  29.4 3.0 %collective-permute-start.11 = (bf16[8,32,128]{2,1,0:T(8,128)(2,1)S(1)}, bf16[8,32,128]{2,1,0:T(8,128)(2,1)S(1)}, u32[]{:S(2)}, u32[]{:S(2)}) collective-permute-start(bf16[8,32,128]{2,1,0:T(8,128)(2,1)S(1)} %get-tuple-element.17.refs_11_), channel_id=1, source_target_pairs={{0,192},{64,128},{128,64},{192,0},{1,193},{65,129},{129,65},{193,1... | collective-permute-start | bytes 196616 | tf_op jit(solution)/shard_map/ppermute | solution.py:257
  32.3 3.3 %collective-permute-done.11.refs_14_ = bf16[8,32,128]{2,1,0:T(8,128)(2,1)S(1)} collective-permute-done((bf16[8,32,128]{2,1,0:T(8,128)(2,1)S(1)}, bf16[8,32,128]{2,1,0:T(8,128)(2,1)S(1)}, u32[]{:S(2)}, u32[]{:S(2)}) %collective-permute-start.11) | collective-permute-done | bytes 65568 | tf_op jit(solution)/shard_map/ppermute | solution.py:257
  35.7 3.3 %sigma.1 = (f32[2,2,128,128]{3,2,1,0:T(8,128)S(1)}, bf16[2,2,128,128]{3,2,1,0:T(8,128)(2,1)S(1)}) custom-call(s32[8,8]{1,0:T(8,128)S(1)} %copy-done.2, s32[4]{0:T(128)S(1)} %copy-done.4, bf16[128,384]{1,0:T(8,128)(2,1)S(1)} %get-tuple-element.15.refs_4_.refs_2_, bf16[544,128]{1,0:T(8,128)(2,1)S(1)} %copy-done.1, ...), custom_call_target="tpu_custom_call" | custom-call | flops 2000000000 | bytes 2000000 | tf_op jit(solution)/shard_map/sigma/pallas_call | solution.py:259
  39.0 0.1 collective-permute-start.12
  39.1 6.2 %collective-permute-done.12 = bf16[2,2,128,128]{3,2,1,0:T(8,128)(2,1)S(1)} collective-permute-done((bf16[2,2,128,128]{3,2,1,0:T(8,128)(2,1)S(1)}, bf16[2,2,128,128]{3,2,1,0:T(8,128)(2,1)S(1)}, u32[]{:S(2)}, u32[]{:S(2)}) %collective-permute-start.12) | collective-permute-done | bytes 131104 | tf_op jit(solution)/shard_map/ppermute | solution.py:276
  45.3 3.4 %collective-permute-start.13 = (bf16[2,2,128,128]{3,2,1,0:T(8,128)(2,1)S(1)}, bf16[2,2,128,128]{3,2,1,0:T(8,128)(2,1)S(1)}, u32[]{:S(2)}, u32[]{:S(2)}) collective-permute-start(bf16[2,2,128,128]{3,2,1,0:T(8,128)(2,1)S(1)} %collective-permute-done.12), channel_id=1, source_target_pairs={{0,64},{64,128},{128,192},{8,72},{72,136},{136,200},{16,80},{80,14... | collective-permute-start | bytes 393224 | tf_op jit(solution)/shard_map/ppermute | solution.py:277
  48.7 11.6 %all_to_all.10 = f32[8,8,128]{2,1,0:T(8,128)S(1)} all-to-all(f32[8,8,128]{2,1,0:T(8,128)S(1)} %get-tuple-element.16), channel_id=1, replica_groups=mesh['sec'=4,'mom'=8,'en'=8] {'mom'}, dimensions={0} | all-to-all | bytes 65536 | tf_op jit(solution)/shard_map/all_to_all | solution.py:255
  60.3 0.7 broadcast_in_dim.12
  60.9 3.6 %all-to-all-start.1 = ((f32[32,8,128]{2,1,0:T(8,128)}), f32[32,8,128]{2,1,0:T(8,128)S(1)}, u32[]{:S(2)}, u32[]{:S(2)}) async-start(f32[32,8,128]{2,1,0:T(8,128)} %broadcast_in_dim.12), calls=%async_computation.1 | async-start | bytes 262144 | tf_op jit(solution)/shard_map/all_to_all | solution.py:280
  64.6 0.6 dynamic_slice.4
  65.8 0.8 %convert_add_fusion = f32[2,2,128,128]{3,2,1,0:T(8,128)} fusion(f32[2,2,128,128]{3,2,1,0:T(8,128)S(1)} %get-tuple-element.18, bf16[2,2,128,128]{3,2,1,0:T(8,128)(2,1)S(1)} %collective-permute-done.13, bf16[2,2,128,128]{3,2,1,0:T(8,128)(2,1)S(1)} %collective-permute-done.12, pred[]{:T(512)S(6)} %eq.9), kind=kLoop, calls=%fused_computation | loop fusion | flops 196608 | bytes 786433 | tf_op jit(solution)/shard_map/add | solution.py:282
  66.6 7.6 %all-to-all-done.1 = f32[32,8,128]{2,1,0:T(8,128)S(1)} async-done(((f32[32,8,128]{2,1,0:T(8,128)}), f32[32,8,128]{2,1,0:T(8,128)S(1)}, u32[]{:S(2)}, u32[]{:S(2)}) %all-to-all-start.1) | async-done | bytes 131104 | tf_op jit(solution)/shard_map/all_to_all | solution.py:280
  74.2 0.6 broadcast_in_dim.14
  (20 shorter events, 0.1 us)
Async XLA Ops:
  0.6 21.1 %copy-start.2 = (s32[8,8]{1,0:T(8,128)S(1)}, s32[8,8]{1,0:T(8,128)}, u32[]{:S(2)}) copy-start(s32[8,8]{1,0:T(8,128)} %refs_0_.5) | copy-start | bytes 772
  0.6 21.1 %copy-start.3 = (bf16[3,128,128]{2,1,0:T(8,128)(2,1)S(1)}, bf16[3,128,128]{2,1,0:T(8,128)(2,1)}, u32[]{:S(2)}) copy-start(bf16[3,128,128]{2,1,0:T(8,128)(2,1)} %refs_1_.2) | copy-start | bytes 294916
  2.4 13.5 %collective-permute-start = (bf16[544,128]{1,0:T(8,128)(2,1)}, bf16[544,128]{1,0:T(8,128)(2,1)S(1)}, u32[]{:S(2)}, u32[]{:S(2)}) collective-permute-start(bf16[544,128]{1,0:T(8,128)(2,1)} %prep.1.refs_4_.refs_5_.refs_3_), channel_id=1, source_target_pairs={{0,7},{1,0},{2,1},{3,2},{4,3},{5,4},{6,5},{7,6},{8,15},{9,8},{10,9... | collective-permute-start | bytes 417800 | tf_op jit(solution)/shard_map/ppermute | solution.py:222
  8.8 7.8 %collective-permute-start.2 = (bf16[544,128]{1,0:T(8,128)(2,1)}, bf16[544,128]{1,0:T(8,128)(2,1)S(1)}, u32[]{:S(2)}, u32[]{:S(2)}) collective-permute-start(bf16[544,128]{1,0:T(8,128)(2,1)} %prep.1.refs_4_.refs_5_.refs_3_), channel_id=1, source_target_pairs={{0,8},{8,0},{16,24},{24,16},{32,40},{40,32},{48,56},{56,48},{1,9},... | collective-permute-start | bytes 417800 | tf_op jit(solution)/shard_map/ppermute | solution.py:221
  11.7 5.3 %collective-permute-start.3 = (bf16[544,128]{1,0:T(8,128)(2,1)}, bf16[544,128]{1,0:T(8,128)(2,1)S(1)}, u32[]{:S(2)}, u32[]{:S(2)}) collective-permute-start(bf16[544,128]{1,0:T(8,128)(2,1)} %prep.1.refs_4_.refs_5_.refs_3_), channel_id=1, source_target_pairs={{0,16},{8,24},{16,32},{24,40},{32,48},{40,56},{48,0},{56,8},{1,17}... | collective-permute-start | bytes 417800 | tf_op jit(solution)/shard_map/ppermute | solution.py:221
  12.9 5.9 %collective-permute-start.4 = (bf16[544,128]{1,0:T(8,128)(2,1)}, bf16[544,128]{1,0:T(8,128)(2,1)S(1)}, u32[]{:S(2)}, u32[]{:S(2)}) collective-permute-start(bf16[544,128]{1,0:T(8,128)(2,1)} %prep.1.refs_4_.refs_5_.refs_3_), channel_id=1, source_target_pairs={{0,48},{8,56},{16,0},{24,8},{32,16},{40,24},{48,32},{56,40},{1,49}... | collective-permute-start | bytes 417800 | tf_op jit(solution)/shard_map/ppermute | solution.py:221
  14.3 7.4 %collective-permute-start.5 = (bf16[544,128]{1,0:T(8,128)(2,1)}, bf16[544,128]{1,0:T(8,128)(2,1)S(1)}, u32[]{:S(2)}, u32[]{:S(2)}) collective-permute-start(bf16[544,128]{1,0:T(8,128)(2,1)} %prep.1.refs_4_.refs_5_.refs_3_), channel_id=1, source_target_pairs={{0,32},{8,40},{16,48},{24,56},{32,0},{40,8},{48,16},{56,24},{1,33}... | collective-permute-start | bytes 417800 | tf_op jit(solution)/shard_map/ppermute | solution.py:221
  15.9 5.9 %collective-permute-start.1 = (bf16[544,128]{1,0:T(8,128)(2,1)S(1)}, bf16[544,128]{1,0:T(8,128)(2,1)S(1)}, u32[]{:S(2)}, u32[]{:S(2)}) collective-permute-start(bf16[544,128]{1,0:T(8,128)(2,1)S(1)} %collective-permute-done.refs_2_), channel_id=1, source_target_pairs={{71,7},{135,71},{199,135},{79,15},{143,79},{207,143},{87,23},{151,... | collective-permute-start | bytes 417800 | tf_op jit(solution)/shard_map/ppermute | solution.py:225
  16.6 8.1 %collective-permute-start.6 = (bf16[544,128]{1,0:T(8,128)(2,1)S(1)}, bf16[544,128]{1,0:T(8,128)(2,1)S(1)}, u32[]{:S(2)}, u32[]{:S(2)}) collective-permute-start(bf16[544,128]{1,0:T(8,128)(2,1)S(1)} %collective-permute-done.2.refs_5_.refs_6_.refs_4_), channel_id=1, source_target_pairs={{0,16},{8,24},{16,32},{24,40},{32,48},{40,56},{48,0},{56,8},{1,17}... | collective-permute-start | bytes 417800 | tf_op jit(solution)/shard_map/ppermute | solution.py:224
  17.0 10.7 %collective-permute-start.7 = (bf16[544,128]{1,0:T(8,128)(2,1)S(1)}, bf16[544,128]{1,0:T(8,128)(2,1)S(1)}, u32[]{:S(2)}, u32[]{:S(2)}) collective-permute-start(bf16[544,128]{1,0:T(8,128)(2,1)S(1)} %collective-permute-done.2.refs_5_.refs_6_.refs_4_), channel_id=1, source_target_pairs={{0,32},{8,40},{16,48},{24,56},{32,0},{40,8},{48,16},{56,24},{1,33}... | collective-permute-start | bytes 417800 | tf_op jit(solution)/shard_map/ppermute | solution.py:224
  18.8 8.9 %collective-permute-start.8 = (bf16[544,128]{1,0:T(8,128)(2,1)S(1)}, bf16[544,128]{1,0:T(8,128)(2,1)S(1)}, u32[]{:S(2)}, u32[]{:S(2)}) collective-permute-start(bf16[544,128]{1,0:T(8,128)(2,1)S(1)} %collective-permute-done.2.refs_5_.refs_6_.refs_4_), channel_id=1, source_target_pairs={{0,48},{8,56},{16,0},{24,8},{32,16},{40,24},{48,32},{56,40},{1,49}... | collective-permute-start | bytes 417800 | tf_op jit(solution)/shard_map/ppermute | solution.py:224
  21.8 0.9 %copy-start = (bf16[544,128]{1,0:T(8,128)(2,1)S(1)}, bf16[544,128]{1,0:T(8,128)(2,1)}, u32[]{:S(2)}) copy-start(bf16[544,128]{1,0:T(8,128)(2,1)} %prep.1.refs_4_.refs_5_.refs_3_) | copy-start | bytes 417796
  22.7 5.1 %copy-start.1 = (bf16[544,128]{1,0:T(8,128)(2,1)S(1)}, bf16[544,128]{1,0:T(8,128)(2,1)}, u32[]{:S(2)}) copy-start(bf16[544,128]{1,0:T(8,128)(2,1)} %prep.1.refs_4_.refs_5_.refs_3_) | copy-start | bytes 417796
  28.9 6.8 %copy-start.4 = (s32[4]{0:T(128)S(1)}, s32[4]{0:T(128)}, u32[]{:S(2)}) copy-start(s32[4]{0:T(128)} %refs_1_.3) | copy-start | bytes 52
  28.9 3.5 %collective-permute-start.10 = (bf16[8,32,128]{2,1,0:T(8,128)(2,1)S(1)}, bf16[8,32,128]{2,1,0:T(8,128)(2,1)S(1)}, u32[]{:S(2)}, u32[]{:S(2)}) collective-permute-start(bf16[8,32,128]{2,1,0:T(8,128)(2,1)S(1)} %get-tuple-element.17.refs_11_), channel_id=1, source_target_pairs={{0,128},{64,192},{128,0},{192,64},{1,129},{65,193},{129,1},{193,65... | collective-permute-start | bytes 196616 | tf_op jit(solution)/shard_map/ppermute | solution.py:257
  29.4 6.3 %collective-permute-start.11 = (bf16[8,32,128]{2,1,0:T(8,128)(2,1)S(1)}, bf16[8,32,128]{2,1,0:T(8,128)(2,1)S(1)}, u32[]{:S(2)}, u32[]{:S(2)}) collective-permute-start(bf16[8,32,128]{2,1,0:T(8,128)(2,1)S(1)} %get-tuple-element.17.refs_11_), channel_id=1, source_target_pairs={{0,192},{64,128},{128,64},{192,0},{1,193},{65,129},{129,65},{193,1... | collective-permute-start | bytes 196616 | tf_op jit(solution)/shard_map/ppermute | solution.py:257
  32.3 3.4 %collective-permute-start.9 = (bf16[8,32,128]{2,1,0:T(8,128)(2,1)S(1)}, bf16[8,32,128]{2,1,0:T(8,128)(2,1)S(1)}, u32[]{:S(2)}, u32[]{:S(2)}) collective-permute-start(bf16[8,32,128]{2,1,0:T(8,128)(2,1)S(1)} %get-tuple-element.17.refs_11_), channel_id=1, source_target_pairs={{0,64},{64,0},{128,192},{192,128},{1,65},{65,1},{129,193},{193,129... | collective-permute-start | bytes 196616 | tf_op jit(solution)/shard_map/ppermute | solution.py:257
  39.0 6.3 %collective-permute-start.12 = (bf16[2,2,128,128]{3,2,1,0:T(8,128)(2,1)S(1)}, bf16[2,2,128,128]{3,2,1,0:T(8,128)(2,1)S(1)}, u32[]{:S(2)}, u32[]{:S(2)}) collective-permute-start(bf16[2,2,128,128]{3,2,1,0:T(8,128)(2,1)S(1)} %get-tuple-element.19), channel_id=1, source_target_pairs={{0,1},{1,2},{2,3},{3,4},{4,5},{5,6},{6,7},{7,0},{8,9},{9,10},{10,1... | collective-permute-start | bytes 393224 | tf_op jit(solution)/shard_map/ppermute | solution.py:276
  45.3 20.6 %collective-permute-start.13 = (bf16[2,2,128,128]{3,2,1,0:T(8,128)(2,1)S(1)}, bf16[2,2,128,128]{3,2,1,0:T(8,128)(2,1)S(1)}, u32[]{:S(2)}, u32[]{:S(2)}) collective-permute-start(bf16[2,2,128,128]{3,2,1,0:T(8,128)(2,1)S(1)} %collective-permute-done.12), channel_id=1, source_target_pairs={{0,64},{64,128},{128,192},{8,72},{72,136},{136,200},{16,80},{80,14... | collective-permute-start | bytes 393224 | tf_op jit(solution)/shard_map/ppermute | solution.py:277
  60.9 13.2 %all-to-all-start.1 = ((f32[32,8,128]{2,1,0:T(8,128)}), f32[32,8,128]{2,1,0:T(8,128)S(1)}, u32[]{:S(2)}, u32[]{:S(2)}) async-start(f32[32,8,128]{2,1,0:T(8,128)} %broadcast_in_dim.12), calls=%async_computation.1 | async-start | bytes 262144 | tf_op jit(solution)/shard_map/all_to_all | solution.py:280

commit v3 on v2

--- a/solution.py
+++ b/solution.py
@@ -252,6 +252,7 @@
         name="late",
         compiler_params=pltpu.CompilerParams(vmem_limit_bytes=6 * 2**20),
     )(momenta, sofar, left, plain, turned, *slots)
+    polar = polar + lax.ppermute(polar, "sec", [(i, i ^ 1) for i in range(4)])
     by_point = lax.all_to_all(polar, "mom", 0, 0, tiled=True)
     modes = [phonon] + [
         lax.ppermute(phonon, "sec", [(i, i ^ d) for i in range(4)]) for d in (1, 2, 3)
@@ -276,8 +277,11 @@
     up = lax.ppermute(rim, "en", [(i, (i + 1) % 8) for i in range(8)])
     over = lax.ppermute(up, ("sec", "en"), [(8 * i, 8 * i + 8) for i in range(3)])
     mine = jnp.sum(by_point, axis=0)
-    copies = jnp.broadcast_to(mine[None], (32,) + mine.shape)
-    spread = lax.all_to_all(copies, ("sec", "en"), 0, 0, tiled=True)
+    copies = jnp.broadcast_to(mine[None], (16,) + mine.shape)
+    groups = [[8 * (core + 2 * far) + e for far in range(2) for e in range(8)] for core in range(2)]
+    spread = lax.all_to_all(
+        copies, ("sec", "en"), 0, 0, axis_index_groups=groups, tiled=True
+    )
     below = jnp.where(lax.axis_index("en") == 0, over, up)
     sigma = own + below.astype(jnp.float32)
     spread, sigma = lax.optimization_barrier((spread, sigma))

time: 75 us -> 75.8 us (1.011)
  blocking collectives: 11.6 us -> 0 us
  waiting for transfers between devices: 22.4 us -> 28.1 us
  starting transfers between devices: 28.3 us -> 34 us
    all_to_all x1 -> x0, blocking collectives: 11.6 us -> none  [per_device(): by_point = lax.all_to_all(polar, 'mom', 0, 0, tiled=True)]
    all_to_all x1 -> x2, starting transfers between devices: 3.64 us -> 9.36 us  [the longest x1 5.88 us: per_device(): by_point = lax.all_to_all(polar, 'mom', 0, 0, tiled=True)]
    all_to_all x1 -> x2, waiting for transfers between devices: 7.55 us -> 11.9 us  [the longest x1 6.58 us: per_device(): lax.all_to_all(copies, ('sec', 'en'), 0, 0, axis_index_groups=groups, til...]
    ppermute x0 -> x1, waiting for transfers between devices: none -> 1.19 us  [per_device(): polar = polar + lax.ppermute(polar, 'sec', [(i, i ^ 1) for i in range(4)])]
  transfers between devices with their start and end apart: 15 -> 17, of which waited for: 6 -> 9; matrix products, arithmetic and copies ran while one was open for 3% -> 3% of each run, Pallas kernels for 2% -> 2%
where the time goes in v3:
time: 75.8 us; the launch traced here: 75.2 us
  starting transfers between devices  34 us (45%)
  waiting for transfers between devices  28.1 us (37%)
  Pallas kernels  7.54 us (10%)
  local copies, waits for them, and re-layouts  2.7 us (4%)
  between operations  1.41 us (2%)
  other arithmetic  1.4 us (2%)
    ppermute x4, starting transfers between devices, per_device(): slots[s] = lax.ppermute(payload, 'mom', mom_pairs(*SHIFTS[s]))  7.12 us
    all_to_all x1, waiting for transfers between devices, per_device(): lax.all_to_all(copies, ('sec', 'en'), 0, 0, axis_index_groups=groups, til...  6.58 us
    ppermute x1, starting transfers between devices, per_device(): along = lax.ppermute(payload, 'en', [(i, (i - 1) % 8) for i in range(8)])  6.39 us
    ppermute x1, waiting for transfers between devices, per_device(): up = lax.ppermute(rim, 'en', [(i, (i + 1) % 8) for i in range(8)])  6.13 us
    all_to_all x1, starting transfers between devices, per_device(): by_point = lax.all_to_all(polar, 'mom', 0, 0, tiled=True)  5.88 us
    all_to_all x1, waiting for transfers between devices, per_device(): by_point = lax.all_to_all(polar, 'mom', 0, 0, tiled=True)  5.33 us
    ppermute x3, waiting for transfers between devices, per_device(): slots[s] = lax.ppermute(slots[1], 'mom', mom_pairs(SHIFTS[s][0], 0))  3.68 us
    ppermute x3, starting transfers between devices, per_device(): lax.ppermute(phonon, 'sec', [(i, i ^ d) for i in range(4)])  3.56 us
  transfers between devices with their start and end apart: 17, of which 9 were waited for; matrix products, arithmetic and copies ran while one was open for 3% of the time, Pallas kernels for 2%

profile of v3, /device:TPU:1, one launch (start us, length us, event | category | flops | bytes accessed | tf_op | source)
XLA Modules:
  0.0 75.2 jit_solution(10647038090230758764)
XLA Ops:
  0.7 1.7 %prep.1.refs_4_.refs_5_.refs_3_ = bf16[544,128]{1,0:T(8,128)(2,1)} custom-call(bf16[4,128,128]{2,1,0:T(8,128)(2,1)} %bitcast.10, f32[3,3,2,128]{3,2,1,0:T(2,128)} %bitcast.11, f32[3,3,2,128]{3,2,1,0:T(2,128)} %bitcast.12), custom_call_target="tpu_custom_call" | custom-call | tf_op jit(solution)/shard_map/prep/pallas_call | solution.py:206
  2.4 6.4 %collective-permute-start = (bf16[544,128]{1,0:T(8,128)(2,1)}, bf16[544,128]{1,0:T(8,128)(2,1)S(1)}, u32[]{:S(2)}, u32[]{:S(2)}) collective-permute-start(bf16[544,128]{1,0:T(8,128)(2,1)} %prep.1.refs_4_.refs_5_.refs_3_), channel_id=1, source_target_pairs={{0,7},{1,0},{2,1},{3,2},{4,3},{5,4},{6,5},{7,6},{8,15},{9,8},{10,9... | collective-permute-start | bytes 417800 | tf_op jit(solution)/shard_map/ppermute | solution.py:222
  8.8 2.9 %collective-permute-start.2 = (bf16[544,128]{1,0:T(8,128)(2,1)}, bf16[544,128]{1,0:T(8,128)(2,1)S(1)}, u32[]{:S(2)}, u32[]{:S(2)}) collective-permute-start(bf16[544,128]{1,0:T(8,128)(2,1)} %prep.1.refs_4_.refs_5_.refs_3_), channel_id=1, source_target_pairs={{0,8},{8,0},{16,24},{24,16},{32,40},{40,32},{48,56},{56,48},{1,9},... | collective-permute-start | bytes 417800 | tf_op jit(solution)/shard_map/ppermute | solution.py:221
  11.7 1.2 %collective-permute-start.3 = (bf16[544,128]{1,0:T(8,128)(2,1)}, bf16[544,128]{1,0:T(8,128)(2,1)S(1)}, u32[]{:S(2)}, u32[]{:S(2)}) collective-permute-start(bf16[544,128]{1,0:T(8,128)(2,1)} %prep.1.refs_4_.refs_5_.refs_3_), channel_id=1, source_target_pairs={{0,16},{8,24},{16,32},{24,40},{32,48},{40,56},{48,0},{56,8},{1,17}... | collective-permute-start | bytes 417800 | tf_op jit(solution)/shard_map/ppermute | solution.py:221
  12.9 1.5 %collective-permute-start.4 = (bf16[544,128]{1,0:T(8,128)(2,1)}, bf16[544,128]{1,0:T(8,128)(2,1)S(1)}, u32[]{:S(2)}, u32[]{:S(2)}) collective-permute-start(bf16[544,128]{1,0:T(8,128)(2,1)} %prep.1.refs_4_.refs_5_.refs_3_), channel_id=1, source_target_pairs={{0,48},{8,56},{16,0},{24,8},{32,16},{40,24},{48,32},{56,40},{1,49}... | collective-permute-start | bytes 417800 | tf_op jit(solution)/shard_map/ppermute | solution.py:221
  14.3 1.5 %collective-permute-start.5 = (bf16[544,128]{1,0:T(8,128)(2,1)}, bf16[544,128]{1,0:T(8,128)(2,1)S(1)}, u32[]{:S(2)}, u32[]{:S(2)}) collective-permute-start(bf16[544,128]{1,0:T(8,128)(2,1)} %prep.1.refs_4_.refs_5_.refs_3_), channel_id=1, source_target_pairs={{0,32},{8,40},{16,48},{24,56},{32,0},{40,8},{48,16},{56,24},{1,33}... | collective-permute-start | bytes 417800 | tf_op jit(solution)/shard_map/ppermute | solution.py:221
  15.9 0.7 collective-permute-start.1
  17.0 1.8 %collective-permute-start.7 = (bf16[544,128]{1,0:T(8,128)(2,1)S(1)}, bf16[544,128]{1,0:T(8,128)(2,1)S(1)}, u32[]{:S(2)}, u32[]{:S(2)}) collective-permute-start(bf16[544,128]{1,0:T(8,128)(2,1)S(1)} %collective-permute-done.2.refs_5_.refs_6_.refs_4_), channel_id=1, source_target_pairs={{0,32},{8,40},{16,48},{24,56},{32,0},{40,8},{48,16},{56,24},{1,33}... | collective-permute-start | bytes 417800 | tf_op jit(solution)/shard_map/ppermute | solution.py:224
  18.8 1.3 %collective-permute-start.8 = (bf16[544,128]{1,0:T(8,128)(2,1)S(1)}, bf16[544,128]{1,0:T(8,128)(2,1)S(1)}, u32[]{:S(2)}, u32[]{:S(2)}) collective-permute-start(bf16[544,128]{1,0:T(8,128)(2,1)S(1)} %collective-permute-done.2.refs_5_.refs_6_.refs_4_), channel_id=1, source_target_pairs={{0,48},{8,56},{16,0},{24,8},{32,16},{40,24},{48,32},{56,40},{1,49}... | collective-permute-start | bytes 417800 | tf_op jit(solution)/shard_map/ppermute | solution.py:224
  20.2 1.6 %collective-permute-done.5.refs_8_.refs_9_.refs_7_ = bf16[544,128]{1,0:T(8,128)(2,1)S(1)} collective-permute-done((bf16[544,128]{1,0:T(8,128)(2,1)}, bf16[544,128]{1,0:T(8,128)(2,1)S(1)}, u32[]{:S(2)}, u32[]{:S(2)}) %collective-permute-start.5) | collective-permute-done | bytes 139296 | tf_op jit(solution)/shard_map/ppermute | solution.py:221
  21.8 0.9 %copy-done = bf16[544,128]{1,0:T(8,128)(2,1)S(1)} copy-done((bf16[544,128]{1,0:T(8,128)(2,1)S(1)}, bf16[544,128]{1,0:T(8,128)(2,1)}, u32[]{:S(2)}) %copy-start) | copy-done | bytes 139288
  22.7 1.4 %early.1 = (f32[8,8,128]{2,1,0:T(8,128)S(1)}, bf16[256,512]{1,0:T(8,128)(2,1)S(1)}, f32[128,384]{1,0:T(8,128)S(1)}, bf16[128,384]{1,0:T(8,128)(2,1)S(1)}) custom-call(s32[8,8]{1,0:T(8,128)S(1)} %copy-done.2, bf16[3,128,128]{2,1,0:T(8,128)(2,1)S(1)} %copy-done.3, bf16[544,128]{1,0:T(8,128)(2,1)S(1)} %collective-permute-done.refs_2_, ...), custom_call_target="tpu_custom_call" | custom-call | flops 1000000000 | bytes 1000000 | tf_op jit(solution)/shard_map/early/pallas_call | solution.py:226
  24.1 0.6 collective-permute-done.6.refs_8_.refs_6_
  24.7 3.1 %collective-permute-done.7.refs_10_.refs_8_ = bf16[544,128]{1,0:T(8,128)(2,1)S(1)} collective-permute-done((bf16[544,128]{1,0:T(8,128)(2,1)S(1)}, bf16[544,128]{1,0:T(8,128)(2,1)S(1)}, u32[]{:S(2)}, u32[]{:S(2)}) %collective-permute-start.7) | collective-permute-done | bytes 139296 | tf_op jit(solution)/shard_map/ppermute | solution.py:224
  27.7 1.1 %late.1 = (f32[8,8,128]{2,1,0:T(8,128)S(1)}, bf16[8,32,128]{2,1,0:T(8,128)(2,1)S(1)}) custom-call(s32[8,8]{1,0:T(8,128)S(1)} %copy-done.2, f32[8,8,128]{2,1,0:T(8,128)S(1)} %get-tuple-element.12.refs_1_, bf16[256,512]{1,0:T(8,128)(2,1)S(1)} %get-tuple-element.13.refs_2_, f32[128,384]{1,0:T(8,128)S(1)} %get-tuple-element.14.refs_3_, ...), custom_call_target="tpu_custom_call" | custom-call | tf_op jit(solution)/shard_map/late/pallas_call | solution.py:243
  28.9 1.8 %collective-permute-start.10 = (bf16[8,32,128]{2,1,0:T(8,128)(2,1)S(1)}, bf16[8,32,128]{2,1,0:T(8,128)(2,1)S(1)}, u32[]{:S(2)}, u32[]{:S(2)}) collective-permute-start(bf16[8,32,128]{2,1,0:T(8,128)(2,1)S(1)} %get-tuple-element.17.refs_11_), channel_id=1, source_target_pairs={{0,64},{64,0},{128,192},{192,128},{1,65},{65,1},{129,193},{193,129... | collective-permute-start | bytes 196616 | tf_op jit(solution)/shard_map/ppermute | solution.py:258
  31.1 1.3 %collective-permute-start.12 = (bf16[8,32,128]{2,1,0:T(8,128)(2,1)S(1)}, bf16[8,32,128]{2,1,0:T(8,128)(2,1)S(1)}, u32[]{:S(2)}, u32[]{:S(2)}) collective-permute-start(bf16[8,32,128]{2,1,0:T(8,128)(2,1)S(1)} %get-tuple-element.17.refs_11_), channel_id=1, source_target_pairs={{0,192},{64,128},{128,64},{192,0},{1,193},{65,129},{129,65},{193,1... | collective-permute-start | bytes 196616 | tf_op jit(solution)/shard_map/ppermute | solution.py:258
  32.4 1.8 %collective-permute-done.11.refs_13_ = bf16[8,32,128]{2,1,0:T(8,128)(2,1)S(1)} collective-permute-done((bf16[8,32,128]{2,1,0:T(8,128)(2,1)S(1)}, bf16[8,32,128]{2,1,0:T(8,128)(2,1)S(1)}, u32[]{:S(2)}, u32[]{:S(2)}) %collective-permute-start.11) | collective-permute-done | bytes 65568 | tf_op jit(solution)/shard_map/ppermute | solution.py:258
  34.2 1.7 %collective-permute-done.12.refs_14_ = bf16[8,32,128]{2,1,0:T(8,128)(2,1)S(1)} collective-permute-done((bf16[8,32,128]{2,1,0:T(8,128)(2,1)S(1)}, bf16[8,32,128]{2,1,0:T(8,128)(2,1)S(1)}, u32[]{:S(2)}, u32[]{:S(2)}) %collective-permute-start.12) | collective-permute-done | bytes 65568 | tf_op jit(solution)/shard_map/ppermute | solution.py:258
  35.9 3.3 %sigma.1 = (f32[2,2,128,128]{3,2,1,0:T(8,128)S(1)}, bf16[2,2,128,128]{3,2,1,0:T(8,128)(2,1)S(1)}) custom-call(s32[8,8]{1,0:T(8,128)S(1)} %copy-done.2, s32[4]{0:T(128)S(1)} %copy-done.4, bf16[128,384]{1,0:T(8,128)(2,1)S(1)} %get-tuple-element.15.refs_4_.refs_2_, bf16[544,128]{1,0:T(8,128)(2,1)S(1)} %copy-done.1, ...), custom_call_target="tpu_custom_call" | custom-call | flops 2000000000 | bytes 2000000 | tf_op jit(solution)/shard_map/sigma/pallas_call | solution.py:260
  39.4 6.1 %collective-permute-done.13 = bf16[2,2,128,128]{3,2,1,0:T(8,128)(2,1)S(1)} collective-permute-done((bf16[2,2,128,128]{3,2,1,0:T(8,128)(2,1)S(1)}, bf16[2,2,128,128]{3,2,1,0:T(8,128)(2,1)S(1)}, u32[]{:S(2)}, u32[]{:S(2)}) %collective-permute-start.13) | collective-permute-done | bytes 131104 | tf_op jit(solution)/shard_map/ppermute | solution.py:277
  45.5 3.2 %collective-permute-start.14 = (bf16[2,2,128,128]{3,2,1,0:T(8,128)(2,1)S(1)}, bf16[2,2,128,128]{3,2,1,0:T(8,128)(2,1)S(1)}, u32[]{:S(2)}, u32[]{:S(2)}) collective-permute-start(bf16[2,2,128,128]{3,2,1,0:T(8,128)(2,1)S(1)} %collective-permute-done.13), channel_id=1, source_target_pairs={{0,64},{64,128},{128,192},{8,72},{72,136},{136,200},{16,80},{80,14... | collective-permute-start | bytes 393224 | tf_op jit(solution)/shard_map/ppermute | solution.py:278
  48.8 1.2 %collective-permute-done.9 = f32[8,8,128]{2,1,0:T(8,128)S(1)} collective-permute-done((f32[8,8,128]{2,1,0:T(8,128)S(1)}, f32[8,8,128]{2,1,0:T(8,128)S(1)}, u32[]{:S(2)}, u32[]{:S(2)}) %collective-permute-start.9) | collective-permute-done | bytes 32800 | tf_op jit(solution)/shard_map/ppermute | solution.py:255
  50.0 0.6 add.10
  50.6 5.9 %all-to-all-start = ((f32[8,8,128]{2,1,0:T(8,128)}), f32[8,8,128]{2,1,0:T(8,128)S(1)}, u32[]{:S(2)}, u32[]{:S(2)}) async-start(f32[8,8,128]{2,1,0:T(8,128)} %add.10), calls=%async_computation | async-start | bytes 65536 | tf_op jit(solution)/shard_map/all_to_all | solution.py:256
  56.5 0.6 dynamic_slice.4
  57.8 5.3 %all-to-all-done = f32[8,8,128]{2,1,0:T(8,128)S(1)} async-done(((f32[8,8,128]{2,1,0:T(8,128)}), f32[8,8,128]{2,1,0:T(8,128)S(1)}, u32[]{:S(2)}, u32[]{:S(2)}) %all-to-all-start) | async-done | bytes 32800 | tf_op jit(solution)/shard_map/all_to_all | solution.py:256
  63.1 0.6 broadcast_in_dim.12
  63.7 3.5 %all-to-all-start.1 = ((f32[16,8,128]{2,1,0:T(8,128)}), f32[16,8,128]{2,1,0:T(8,128)S(1)}, u32[]{:S(2)}, u32[]{:S(2)}) async-start(f32[16,8,128]{2,1,0:T(8,128)} %broadcast_in_dim.12), calls=%async_computation.1 | async-start | bytes 131072 | tf_op jit(solution)/shard_map/all_to_all | solution.py:282
  67.2 0.7 convert_add_fusion
  68.0 6.6 %all-to-all-done.1 = f32[16,8,128]{2,1,0:T(8,128)S(1)} async-done(((f32[16,8,128]{2,1,0:T(8,128)}), f32[16,8,128]{2,1,0:T(8,128)S(1)}, u32[]{:S(2)}, u32[]{:S(2)}) %all-to-all-start.1) | async-done | bytes 65568 | tf_op jit(solution)/shard_map/all_to_all | solution.py:282
  74.6 0.6 broadcast_in_dim.14
  (24 shorter events, 1.1 us)
Async XLA Ops:
  0.6 21.1 %copy-start.2 = (s32[8,8]{1,0:T(8,128)S(1)}, s32[8,8]{1,0:T(8,128)}, u32[]{:S(2)}) copy-start(s32[8,8]{1,0:T(8,128)} %refs_0_.5) | copy-start | bytes 772
  0.6 21.1 %copy-start.3 = (bf16[3,128,128]{2,1,0:T(8,128)(2,1)S(1)}, bf16[3,128,128]{2,1,0:T(8,128)(2,1)}, u32[]{:S(2)}) copy-start(bf16[3,128,128]{2,1,0:T(8,128)(2,1)} %refs_1_.2) | copy-start | bytes 294916
  2.4 13.5 %collective-permute-start = (bf16[544,128]{1,0:T(8,128)(2,1)}, bf16[544,128]{1,0:T(8,128)(2,1)S(1)}, u32[]{:S(2)}, u32[]{:S(2)}) collective-permute-start(bf16[544,128]{1,0:T(8,128)(2,1)} %prep.1.refs_4_.refs_5_.refs_3_), channel_id=1, source_target_pairs={{0,7},{1,0},{2,1},{3,2},{4,3},{5,4},{6,5},{7,6},{8,15},{9,8},{10,9... | collective-permute-start | bytes 417800 | tf_op jit(solution)/shard_map/ppermute | solution.py:222
  8.8 7.8 %collective-permute-start.2 = (bf16[544,128]{1,0:T(8,128)(2,1)}, bf16[544,128]{1,0:T(8,128)(2,1)S(1)}, u32[]{:S(2)}, u32[]{:S(2)}) collective-permute-start(bf16[544,128]{1,0:T(8,128)(2,1)} %prep.1.refs_4_.refs_5_.refs_3_), channel_id=1, source_target_pairs={{0,8},{8,0},{16,24},{24,16},{32,40},{40,32},{48,56},{56,48},{1,9},... | collective-permute-start | bytes 417800 | tf_op jit(solution)/shard_map/ppermute | solution.py:221
  11.7 5.3 %collective-permute-start.3 = (bf16[544,128]{1,0:T(8,128)(2,1)}, bf16[544,128]{1,0:T(8,128)(2,1)S(1)}, u32[]{:S(2)}, u32[]{:S(2)}) collective-permute-start(bf16[544,128]{1,0:T(8,128)(2,1)} %prep.1.refs_4_.refs_5_.refs_3_), channel_id=1, source_target_pairs={{0,16},{8,24},{16,32},{24,40},{32,48},{40,56},{48,0},{56,8},{1,17}... | collective-permute-start | bytes 417800 | tf_op jit(solution)/shard_map/ppermute | solution.py:221
  12.9 5.9 %collective-permute-start.4 = (bf16[544,128]{1,0:T(8,128)(2,1)}, bf16[544,128]{1,0:T(8,128)(2,1)S(1)}, u32[]{:S(2)}, u32[]{:S(2)}) collective-permute-start(bf16[544,128]{1,0:T(8,128)(2,1)} %prep.1.refs_4_.refs_5_.refs_3_), channel_id=1, source_target_pairs={{0,48},{8,56},{16,0},{24,8},{32,16},{40,24},{48,32},{56,40},{1,49}... | collective-permute-start | bytes 417800 | tf_op jit(solution)/shard_map/ppermute | solution.py:221
  14.3 7.4 %collective-permute-start.5 = (bf16[544,128]{1,0:T(8,128)(2,1)}, bf16[544,128]{1,0:T(8,128)(2,1)S(1)}, u32[]{:S(2)}, u32[]{:S(2)}) collective-permute-start(bf16[544,128]{1,0:T(8,128)(2,1)} %prep.1.refs_4_.refs_5_.refs_3_), channel_id=1, source_target_pairs={{0,32},{8,40},{16,48},{24,56},{32,0},{40,8},{48,16},{56,24},{1,33}... | collective-permute-start | bytes 417800 | tf_op jit(solution)/shard_map/ppermute | solution.py:221
  15.9 5.9 %collective-permute-start.1 = (bf16[544,128]{1,0:T(8,128)(2,1)S(1)}, bf16[544,128]{1,0:T(8,128)(2,1)S(1)}, u32[]{:S(2)}, u32[]{:S(2)}) collective-permute-start(bf16[544,128]{1,0:T(8,128)(2,1)S(1)} %collective-permute-done.refs_2_), channel_id=1, source_target_pairs={{71,7},{135,71},{199,135},{79,15},{143,79},{207,143},{87,23},{151,... | collective-permute-start | bytes 417800 | tf_op jit(solution)/shard_map/ppermute | solution.py:225
  16.6 8.1 %collective-permute-start.6 = (bf16[544,128]{1,0:T(8,128)(2,1)S(1)}, bf16[544,128]{1,0:T(8,128)(2,1)S(1)}, u32[]{:S(2)}, u32[]{:S(2)}) collective-permute-start(bf16[544,128]{1,0:T(8,128)(2,1)S(1)} %collective-permute-done.2.refs_5_.refs_6_.refs_4_), channel_id=1, source_target_pairs={{0,16},{8,24},{16,32},{24,40},{32,48},{40,56},{48,0},{56,8},{1,17}... | collective-permute-start | bytes 417800 | tf_op jit(solution)/shard_map/ppermute | solution.py:224
  17.0 10.7 %collective-permute-start.7 = (bf16[544,128]{1,0:T(8,128)(2,1)S(1)}, bf16[544,128]{1,0:T(8,128)(2,1)S(1)}, u32[]{:S(2)}, u32[]{:S(2)}) collective-permute-start(bf16[544,128]{1,0:T(8,128)(2,1)S(1)} %collective-permute-done.2.refs_5_.refs_6_.refs_4_), channel_id=1, source_target_pairs={{0,32},{8,40},{16,48},{24,56},{32,0},{40,8},{48,16},{56,24},{1,33}... | collective-permute-start | bytes 417800 | tf_op jit(solution)/shard_map/ppermute | solution.py:224
  18.8 8.9 %collective-permute-start.8 = (bf16[544,128]{1,0:T(8,128)(2,1)S(1)}, bf16[544,128]{1,0:T(8,128)(2,1)S(1)}, u32[]{:S(2)}, u32[]{:S(2)}) collective-permute-start(bf16[544,128]{1,0:T(8,128)(2,1)S(1)} %collective-permute-done.2.refs_5_.refs_6_.refs_4_), channel_id=1, source_target_pairs={{0,48},{8,56},{16,0},{24,8},{32,16},{40,24},{48,32},{56,40},{1,49}... | collective-permute-start | bytes 417800 | tf_op jit(solution)/shard_map/ppermute | solution.py:224
  21.8 0.9 %copy-start = (bf16[544,128]{1,0:T(8,128)(2,1)S(1)}, bf16[544,128]{1,0:T(8,128)(2,1)}, u32[]{:S(2)}) copy-start(bf16[544,128]{1,0:T(8,128)(2,1)} %prep.1.refs_4_.refs_5_.refs_3_) | copy-start | bytes 417796
  22.7 5.1 %copy-start.1 = (bf16[544,128]{1,0:T(8,128)(2,1)S(1)}, bf16[544,128]{1,0:T(8,128)(2,1)}, u32[]{:S(2)}) copy-start(bf16[544,128]{1,0:T(8,128)(2,1)} %prep.1.refs_4_.refs_5_.refs_3_) | copy-start | bytes 417796
  28.9 7.1 %copy-start.4 = (s32[4]{0:T(128)S(1)}, s32[4]{0:T(128)}, u32[]{:S(2)}) copy-start(s32[4]{0:T(128)} %refs_1_.3) | copy-start | bytes 52
  28.9 3.6 %collective-permute-start.10 = (bf16[8,32,128]{2,1,0:T(8,128)(2,1)S(1)}, bf16[8,32,128]{2,1,0:T(8,128)(2,1)S(1)}, u32[]{:S(2)}, u32[]{:S(2)}) collective-permute-start(bf16[8,32,128]{2,1,0:T(8,128)(2,1)S(1)} %get-tuple-element.17.refs_11_), channel_id=1, source_target_pairs={{0,64},{64,0},{128,192},{192,128},{1,65},{65,1},{129,193},{193,129... | collective-permute-start | bytes 196616 | tf_op jit(solution)/shard_map/ppermute | solution.py:258
  30.7 3.5 %collective-permute-start.11 = (bf16[8,32,128]{2,1,0:T(8,128)(2,1)S(1)}, bf16[8,32,128]{2,1,0:T(8,128)(2,1)S(1)}, u32[]{:S(2)}, u32[]{:S(2)}) collective-permute-start(bf16[8,32,128]{2,1,0:T(8,128)(2,1)S(1)} %get-tuple-element.17.refs_11_), channel_id=1, source_target_pairs={{0,128},{64,192},{128,0},{192,64},{1,129},{65,193},{129,1},{193,65... | collective-permute-start | bytes 196616 | tf_op jit(solution)/shard_map/ppermute | solution.py:258
  31.1 4.8 %collective-permute-start.12 = (bf16[8,32,128]{2,1,0:T(8,128)(2,1)S(1)}, bf16[8,32,128]{2,1,0:T(8,128)(2,1)S(1)}, u32[]{:S(2)}, u32[]{:S(2)}) collective-permute-start(bf16[8,32,128]{2,1,0:T(8,128)(2,1)S(1)} %get-tuple-element.17.refs_11_), channel_id=1, source_target_pairs={{0,192},{64,128},{128,64},{192,0},{1,193},{65,129},{129,65},{193,1... | collective-permute-start | bytes 196616 | tf_op jit(solution)/shard_map/ppermute | solution.py:258
  39.3 6.2 %collective-permute-start.13 = (bf16[2,2,128,128]{3,2,1,0:T(8,128)(2,1)S(1)}, bf16[2,2,128,128]{3,2,1,0:T(8,128)(2,1)S(1)}, u32[]{:S(2)}, u32[]{:S(2)}) collective-permute-start(bf16[2,2,128,128]{3,2,1,0:T(8,128)(2,1)S(1)} %get-tuple-element.19), channel_id=1, source_target_pairs={{0,1},{1,2},{2,3},{3,4},{4,5},{5,6},{6,7},{7,0},{8,9},{9,10},{10,1... | collective-permute-start | bytes 393224 | tf_op jit(solution)/shard_map/ppermute | solution.py:277
  45.5 21.7 %collective-permute-start.14 = (bf16[2,2,128,128]{3,2,1,0:T(8,128)(2,1)S(1)}, bf16[2,2,128,128]{3,2,1,0:T(8,128)(2,1)S(1)}, u32[]{:S(2)}, u32[]{:S(2)}) collective-permute-start(bf16[2,2,128,128]{3,2,1,0:T(8,128)(2,1)S(1)} %collective-permute-done.13), channel_id=1, source_target_pairs={{0,64},{64,128},{128,192},{8,72},{72,136},{136,200},{16,80},{80,14... | collective-permute-start | bytes 393224 | tf_op jit(solution)/shard_map/ppermute | solution.py:278
  48.7 1.3 %collective-permute-start.9 = (f32[8,8,128]{2,1,0:T(8,128)S(1)}, f32[8,8,128]{2,1,0:T(8,128)S(1)}, u32[]{:S(2)}, u32[]{:S(2)}) collective-permute-start(f32[8,8,128]{2,1,0:T(8,128)S(1)} %get-tuple-element.16), channel_id=1, source_target_pairs={{0,64},{64,0},{128,192},{192,128},{1,65},{65,1},{129,193},{193,129... | collective-permute-start | bytes 98312 | tf_op jit(solution)/shard_map/ppermute | solution.py:255
  50.6 12.4 %all-to-all-start = ((f32[8,8,128]{2,1,0:T(8,128)}), f32[8,8,128]{2,1,0:T(8,128)S(1)}, u32[]{:S(2)}, u32[]{:S(2)}) async-start(f32[8,8,128]{2,1,0:T(8,128)} %add.10), calls=%async_computation | async-start | bytes 65536 | tf_op jit(solution)/shard_map/all_to_all | solution.py:256
  63.7 10.8 %all-to-all-start.1 = ((f32[16,8,128]{2,1,0:T(8,128)}), f32[16,8,128]{2,1,0:T(8,128)S(1)}, u32[]{:S(2)}, u32[]{:S(2)}) async-start(f32[16,8,128]{2,1,0:T(8,128)} %broadcast_in_dim.12), calls=%async_computation.1 | async-start | bytes 131072 | tf_op jit(solution)/shard_map/all_to_all | solution.py:282
